TPU v7x, 32 devices: a whole 2x2x4 slice. The times are simulated.
32 devices in a mesh: box: 2 (over core), row: 16 (over z, y, x).
Axes of the slice: x: 2, y: 2, z: 4, core: 2. Of those that a mesh axis runs over, the one named last changes fastest.
Arguments:
- dtn: float32 [4, 6, 384, 2304], P('box', None, 'row'), may hold values from -2 to 8, as said below
- interface_perm: int32 [2, 384], P('box'), may hold values from 0 to 383, each once within a row
Outputs:
- solution_first: float32 [2, 384, 3840], P('box', 'row')
- solution_second: float32 [2, 384, 6144], P('box', 'row')
- merged_map: float32 [2, 8, 384, 6144], P('box', None, 'row')
Inputs may be any that keep to these rules, and one draw needn't show every extreme that they name: `dtn`: each box's map, read as a (2304) x (2304) matrix, is symmetric and positive definite.
All inputs are finite; a program needn't handle non-finite values.
Results may differ from a plain program's by a relative error of at most 0.00012.
Values sent between devices are 32-bit elements; how exact they have to be, the bound alone decides.
A program may use at most 192 MiB of HBM per device.

v0:
```python
import functools

import jax
import jax.numpy as jnp
from jax import lax
from jax.experimental import pallas as pl
from jax.experimental.pallas import tpu as pltpu
from jax.sharding import PartitionSpec as P

HIGHEST = lax.Precision.HIGHEST
HIGH = lax.Precision.HIGH
BLOCK = 128
GROUP = 4


def dot(left, right, precision=HIGHEST):
    return jnp.dot(left, right, precision=precision, preferred_element_type=jnp.float32)


def dot_t(left, right):
    return lax.dot_general(
        left, right, (((0,), (0,)), ((), ())), precision=HIGHEST, preferred_element_type=jnp.float32
    )


def invert_block(blk):
    size = blk.shape[0]
    lane = lax.broadcasted_iota(jnp.int32, (1, size), 1)

    def step(g, carry):
        k = g * GROUP
        full = blk[...]
        cols = [
            jnp.take_along_axis(full, jnp.full((size, size), k + i, jnp.int32), axis=1)
            for i in range(GROUP)
        ]
        rows = [blk[pl.ds(k + i, 1), :] for i in range(GROUP)]
        wide = [jnp.broadcast_to(r, (8, size)) for r in rows]
        pivots = [
            [
                jnp.take_along_axis(wide[i], jnp.full((8, size), k + j, jnp.int32), axis=1)
                for j in range(GROUP)
            ]
            for i in range(GROUP)
        ]
        inside = (lane >= k) & (lane < k + GROUP)
        wide = [
            jnp.where(lane == k + i, 1.0, jnp.where(inside, 0.0, wide[i])) for i in range(GROUP)
        ]
        for i in range(GROUP):
            p = 1.0 / pivots[i][i]
            wide[i] = wide[i] * p
            for j in range(i + 1, GROUP):
                pivots[i][j] = pivots[i][j] * p
            for l in range(GROUP):
                if l != i:
                    f = pivots[l][i]
                    wide[l] = wide[l] - f * wide[i]
                    for j in range(i + 1, GROUP):
                        pivots[l][j] = pivots[l][j] - f * pivots[i][j]
        result = jnp.where(inside, 0.0, full)
        for i in range(GROUP):
            result = result - cols[i] * wide[i][0:1]
        blk[...] = result
        for i in range(GROUP):
            blk[pl.ds(k + i, 1), :] = wide[i][0:1]
        return carry

    lax.fori_loop(0, size // GROUP, step, 0)


def invert(mat, blk, col):
    order = mat.shape[0]
    count = order // BLOCK
    eye = (
        lax.broadcasted_iota(jnp.int32, (BLOCK, BLOCK), 0)
        == lax.broadcasted_iota(jnp.int32, (BLOCK, BLOCK), 1)
    ).astype(jnp.float32)

    def outer(j, carry):
        here = pl.ds(pl.multiple_of(j * BLOCK, BLOCK), BLOCK)
        blk[...] = mat[here, here]
        invert_block(blk)
        col[...] = mat[:, here]
        mat[:, here] = jnp.zeros((order, BLOCK), jnp.float32)
        mat[here, here] = eye
        col[here, :] = jnp.zeros((BLOCK, BLOCK), jnp.float32)
        mat[here, :] = dot(blk[...], mat[here, :])

        def inner(i, c):
            there = pl.ds(pl.multiple_of(i * BLOCK, BLOCK), BLOCK)
            mat[there, :] = mat[there, :] - dot(col[there, :], mat[here, :])
            return c

        @pl.loop(0, count)
        def _(i):
            @pl.when(i != j)
            def _():
                inner(i, 0)

        return carry

    lax.fori_loop(0, count, outer, 0)


def first_kernel(perm_ref, small_ref, inv_ref, coupled_ref, own_ref, mat, blk, col):
    f = mat.shape[0]
    count = f // BLOCK

    def block(ref, i):
        return ref[:, i * f : (i + 1) * f]

    def place(rows):
        return (
            perm_ref[rows, :] == lax.broadcasted_iota(jnp.int32, (BLOCK, f), 1)
        ).astype(jnp.float32)

    whole = (perm_ref[...] == lax.broadcasted_iota(jnp.int32, (f, f), 1)).astype(jnp.float32)

    @pl.loop(0, count)
    def _(i):
        here = pl.ds(pl.multiple_of(i * BLOCK, BLOCK), BLOCK)
        moved = dot(place(here), block(small_ref, 1))
        mat[here, :] = small_ref[here, :f] + lax.dot_general(
            moved,
            whole,
            (((1,), (1,)), ((), ())),
            precision=HIGHEST,
            preferred_element_type=jnp.float32,
        )

    invert(mat, blk, col)

    @pl.loop(0, count)
    def _(i):
        here = pl.ds(pl.multiple_of(i * BLOCK, BLOCK), BLOCK)
        inv_ref[here, :f] = mat[here, :]
        inv_ref[here, f:] = dot(mat[here, :], whole)

    @pl.loop(0, count)
    def _(i):
        there = pl.ds(pl.multiple_of(f + i * BLOCK, BLOCK), BLOCK)
        picked = (
            perm_ref[...] == lax.broadcasted_iota(jnp.int32, (f, BLOCK), 1) + i * BLOCK
        ).astype(jnp.float32)
        inv_ref[there, :] = dot_t(picked, inv_ref[:f, :])

    for h in range(2):

        @pl.loop(0, count)
        def _(i):
            here = pl.ds(pl.multiple_of(i * BLOCK, BLOCK), BLOCK)
            rows = pl.ds(pl.multiple_of(h * f + i * BLOCK, BLOCK), BLOCK)
            edge = small_ref[:, pl.ds(pl.multiple_of((2 + h) * f + i * BLOCK, BLOCK), BLOCK)]
            coupled_ref[rows, :] = -dot_t(edge, inv_ref[h * f : (h + 1) * f, :])
            for c in range(2):
                value = dot(coupled_ref[rows, c * f : (c + 1) * f], block(small_ref, 2 + c))
                if c == h:
                    value = value + small_ref[here, (4 + h) * f : (5 + h) * f]
                own_ref[rows, c * f : (c + 1) * f] = value


def second_kernel(own_ref, part_ref, lift_ref, pick_ref, out_ref, mat, blk, col):
    mat[...] = own_ref[...] + part_ref[...]
    invert(mat, blk, col)
    n = lift_ref.shape[0]
    out_ref[:n, :] = dot(lift_ref[...], mat[...])
    out_ref[n:, :] = dot(pick_ref[...], mat[...])


def flip(index, bit):
    return index + bit - 2 * bit * ((index // bit) % 2)


def plan(n, width):
    bits = []
    bit = n // 2
    while bit:
        bits.append(bit)
        bit //= 2
    tiles = width // 128
    first = tiles * 3 // 8
    second = tiles * 3 // 8 + (tiles * 3 % 8 >= 4)
    orders = [bits, bits[:-2] + [1, 2], [1, 2] + bits[:-2]]
    sizes = [first, second, tiles - first - second]
    chunks, at = [], 0
    for order, size in zip(orders, sizes):
        chunks.append((at * 128, size * 128, order))
        at += size
    return bits, chunks


def gather_kernel(n, bits, chunks, x_ref, out_ref, send_sem, recv_sem, own_sem):
    me = lax.axis_index("row")
    barrier = pltpu.get_barrier_semaphore()
    for bit in bits:
        pl.semaphore_signal(
            barrier, inc=1, device_id={"row": flip(me, bit)}, device_id_type=pl.DeviceIdType.MESH
        )
    local = pltpu.make_async_copy(x_ref, out_ref.at[me], own_sem)
    local.start()
    local.wait()
    pl.semaphore_wait(barrier, len(bits))
    pending = [[] for _ in chunks]
    sent = []
    held = [[()] for _ in chunks]
    for t in range(len(bits)):
        for c, (start, size, order) in enumerate(chunks):
            for copy in pending[c]:
                copy.wait_recv()
            pending[c] = []
            bit = order[t]
            for s in held[c]:
                slot = me
                for one in s:
                    slot = flip(slot, one)
                number = (1 << t) - 1 + len(pending[c])
                piece = out_ref.at[slot, :, pl.ds(start, size)]
                copy = pltpu.make_async_remote_copy(
                    src_ref=piece,
                    dst_ref=piece,
                    send_sem=send_sem.at[c, number],
                    recv_sem=recv_sem.at[c, number],
                    device_id={"row": flip(me, bit)},
                    device_id_type=pl.DeviceIdType.MESH,
                )
                copy.start()
                pending[c].append(copy)
                sent.append(copy)
            held[c] = held[c] + [s + (bit,) for s in held[c]]
    for c in range(len(chunks)):
        for copy in pending[c]:
            copy.wait_recv()
    for copy in sent:
        copy.wait_send()


def quick_gather(x):
    n = lax.axis_size("row")
    count, width = x.shape
    bits, chunks = plan(n, width)
    out = pl.pallas_call(
        functools.partial(gather_kernel, n, bits, chunks),
        out_shape=jax.ShapeDtypeStruct((n, count, width), jnp.float32),
        in_specs=[pl.BlockSpec(memory_space=pltpu.VMEM)],
        out_specs=pl.BlockSpec(memory_space=pltpu.VMEM),
        scratch_shapes=[
            pltpu.SemaphoreType.DMA((len(chunks), n - 1)),
            pltpu.SemaphoreType.DMA((len(chunks), n - 1)),
            pltpu.SemaphoreType.DMA,
        ],
        compiler_params=pltpu.CompilerParams(
            collective_id=0, has_side_effects=True, vmem_limit_bytes=16 * 1024 * 1024
        ),
        cost_estimate=pl.CostEstimate(
            flops=10_000_000_000, bytes_accessed=2 * n * count * width * 4, transcendentals=0
        ),
    )(x)
    return out.reshape(n * count, width)


def call(kernel, out, order, *args):
    return pl.pallas_call(
        kernel,
        out_shape=[jax.ShapeDtypeStruct(o, jnp.float32) for o in out],
        in_specs=[pl.BlockSpec(memory_space=pltpu.VMEM)] * len(args),
        out_specs=[pl.BlockSpec(memory_space=pltpu.VMEM)] * len(out),
        scratch_shapes=[
            pltpu.VMEM((order, order), jnp.float32),
            pltpu.VMEM((BLOCK, BLOCK), jnp.float32),
            pltpu.VMEM((order, BLOCK), jnp.float32),
        ],
        compiler_params=pltpu.CompilerParams(vmem_limit_bytes=40 * 1024 * 1024),
        cost_estimate=pl.CostEstimate(
            flops=order * 20_000_000, bytes_accessed=order * order * 8, transcendentals=0
        ),
    )(*args)


def body(dtn, interface_perm):
    a, b = dtn[0], dtn[1]
    count = a.shape[1]
    f = a.shape[2] // 6
    perm = interface_perm[0]
    rank = lax.axis_index("row")
    half = lax.axis_index("box") % 2
    first = half == 0

    def swap(x):
        n = lax.axis_size("box")
        return lax.ppermute(x, "box", [(i, i ^ 1) for i in range(n)])

    def gather(x):
        return lax.all_gather(x, "row", axis=0, tiled=True)

    def cols(x, face):
        return x[..., face * f : (face + 1) * f]

    def side(x):
        return jnp.where(first, cols(x, 3), cols(x, 2))

    def free(x):
        return jnp.where(first, cols(x, 2), cols(x, 3))

    def outer_cols(x, edge):
        return jnp.concatenate([cols(x, edge), free(x), cols(x, 4), cols(x, 5)], axis=-1)

    ay, by = jnp.where(first, a[3], a[2]), jnp.where(first, b[3], b[2])
    a1, b0 = a[1], b[0]
    small = quick_gather(
        jnp.concatenate(
            [cols(a1, 1), cols(b0, 0), side(a1), side(b0), side(ay), side(by)], axis=1
        )
    )
    bulk = gather(
        jnp.concatenate(
            [outer_cols(a1, 0), outer_cols(ay, 0), outer_cols(b0, 1), outer_cols(by, 1)], axis=1
        )
    )
    inv1, coupled, own_ss = call(first_kernel, [(2 * f, 2 * f)] * 3, f, perm[:, None], small)
    a1y, b0y = small[:, 2 * f : 3 * f], small[:, 3 * f : 4 * f]

    def times_side(x):
        return jnp.concatenate([dot(x[:, :f], a1y), dot(x[:, f:], b0y)], axis=1)

    part_ss = swap(own_ss)
    outer_a = jnp.concatenate(
        [a[0], jnp.where(first, a[2], a[3]), a[4], a[5]], axis=0
    )
    outer_b = jnp.concatenate(
        [b[1], jnp.where(first, b[2], b[3]), b[4], b[5]], axis=0
    )
    lift = -jnp.concatenate(
        [dot(cols(outer_a, 1), inv1[:f]), dot(cols(outer_b, 0), inv1[f:])], axis=0
    )
    n = 4 * count
    zero_n = jnp.zeros((n, f), jnp.float32)
    lift_two = times_side(lift) + jnp.concatenate(
        [
            jnp.concatenate([side(outer_a), zero_n], axis=1),
            jnp.concatenate([zero_n, side(outer_b)], axis=1),
        ],
        axis=0,
    )
    start = rank * count
    pick = (
        jnp.arange(2 * f, dtype=jnp.int32)[None, :]
        == half * f + start + jnp.arange(count, dtype=jnp.int32)[:, None]
    ).astype(jnp.float32)
    own_rows = lax.dynamic_slice(inv1, (start, 0), (count, 2 * f))
    z = -call(second_kernel, [(2 * n + count, 2 * f)], 2 * f, own_ss, part_ss, lift_two, pick)[0]
    z_part = swap(z)
    both = jnp.concatenate([z_part, z], axis=0)
    through = dot(both, coupled)
    m = 2 * n + count
    through = jnp.concatenate(
        [through[:m], through[m : m + 2 * n] + lift, through[m + 2 * n :], -own_rows], axis=0
    )
    both = jnp.concatenate([both, jnp.zeros((count, 2 * f), jnp.float32)], axis=0)
    w = 4 * f
    res_a = dot(through[:, :f], bulk[:, :w], HIGH) + dot(both[:, :f], bulk[:, w : 2 * w], HIGH)
    res_b = dot(through[:, f:], bulk[:, 2 * w : 3 * w], HIGH) + dot(both[:, f:], bulk[:, 3 * w :], HIGH)
    results = jnp.concatenate([res_a, res_b], axis=1)
    cross = swap(results[:m])
    own = results[m : 2 * m]
    base = jnp.concatenate(
        [
            jnp.concatenate([outer_cols(outer_a, 0), jnp.zeros((n, w), jnp.float32)], axis=1),
            jnp.concatenate([jnp.zeros((n, w), jnp.float32), outer_cols(outer_b, 1)], axis=1),
        ],
        axis=0,
    )
    own_map = own[: 2 * n] + base
    left = jnp.where(first, own_map, cross[: 2 * n])
    right = jnp.where(first, cross[: 2 * n], own_map)
    merged_map = jnp.concatenate([left, right], axis=1).reshape(1, 8, count, 4 * w)
    own_s, cross_s = own[2 * n :], cross[2 * n :]
    second = jnp.concatenate(
        [jnp.where(first, own_s, cross_s), jnp.where(first, cross_s, own_s)], axis=1
    )
    s1 = results[2 * m :]
    y_a, y_b = -dot(own_rows[:, :f], a1y), -dot(own_rows[:, f:], b0y)

    def ordered(x, y):
        two = jnp.where(first, cols(x, 1), y)
        three = jnp.where(first, y, cols(x, 1))
        return [cols(x, 0), two, three, x[:, 2 * f :]]

    solution_first = jnp.concatenate(ordered(s1[:, :w], y_a) + ordered(s1[:, w:], y_b), axis=1)
    return (solution_first[None], second[None], merged_map)


def solution(mesh):
    return jax.shard_map(
        body,
        mesh=mesh,
        in_specs=(P("box", None, "row", None), P("box", None)),
        out_specs=(P("box", "row", None), P("box", "row", None), P("box", None, "row", None)),
        check_vma=False,
    )
```

profile of v0, /device:TPU:15, one launch (start us, length us, event | category | flops | bytes accessed | tf_op | source)
XLA Modules:
  0.0 247.7 jit_solution(9287584035761696775)
XLA Ops:
  7.2 0.0 all-gather.2.cloned.1.call-start
  7.2 2.8 %slice_bitcast_fusion.5 = (f32[24,2304]{1,0:T(8,128)S(1)}, f32[24,2304]{1,0:T(8,128)S(1)}, f32[24,2304]{1,0:T(8,128)S(1)}, f32[24,2304]{1,0:T(8,128)S(1)}, f32[2...) fusion(f32[2,6,24,2304]{3,2,1,0:T(8,128)} %param.2, ...), kind=kLoop, calls=%fused_computation.86 | loop fusion | flops 221184 | bytes 5308417 | tf_op jit(solution)/shard_map/squeeze | solution.py:328
  10.1 0.0 copy-start.28
  10.3 0.0 copy-start.24
  10.3 0.8 copy-done.24
  11.1 0.0 all-gather.2.cloned.1.call-update
  11.2 0.0 copy-done.28
  11.2 0.1 copy.5.perm_ref
  11.3 58.9 %shard_map.49 = f32[16,24,2304]{2,1,0:T(8,128)S(1)} custom-call(f32[24,2304]{1,0:T(8,128)S(1)} %get-tuple-element.31.x_ref), custom_call_target="tpu_custom_call" | custom-call | flops 10000000000 | bytes 7077888 | tf_op jit(solution)/shard_map/pallas_call | solution.py:242
  70.2 0.0 copy-start.1
  70.2 43.0 %shard_map.50 = (f32[768,768]{1,0:T(8,128)S(1)}, f32[768,768]{1,0:T(8,128)S(1)}, f32[768,768]{1,0:T(8,128)}) custom-call(s32[384,1]{1,0:T(8,128)S(1)} %copy.5.perm_ref, f32[384,2304]{1,0:T(8,128)S(1)} %bitcast.31), custom_call_target="tpu_custom_call" | custom-call | flops 7680000000 | bytes 1179648 | tf_op jit(solution)/shard_map/pallas_call | solution.py:263
  113.2 0.0 copy-done.1
  113.2 1.4 copy-done
  114.6 4.4 %collective-permute-start = (f32[768,768]{1,0:T(8,128)}, f32[768,768]{1,0:T(8,128)}, u32[]{:S(2)}, u32[]{:S(2)}) collective-permute-start(f32[768,768]{1,0:T(8,128)} %get-tuple-element.6.own_ref), channel_id=1, source_target_pairs={{0,16},{16,0},{1,17},{17,1},{2,18},{18,2},{3,19},{19,3},{4,20},{20... | collective-permute-start | bytes 7077896 | tf_op jit(solution)/shard_map/ppermute | solution.py:291
  119.0 1.6 fusion.24
  120.7 1.8 fusion.22
  122.5 0.0 copy-start.22
  122.5 0.7 copy-done.22
  123.3 0.8 broadcast_select_fusion
  124.2 1.8 fusion.35
  126.0 1.8 fusion.32
  127.8 0.1 fusion.30.lift_ref
  127.9 0.1 fusion.53.pick_ref
  128.0 0.0 collective-permute-done.part_ref
  128.0 62.1 %shard_map.51 = f32[216,768]{1,0:T(8,128)S(1)} custom-call(f32[768,768]{1,0:T(8,128)} %get-tuple-element.6.own_ref, f32[768,768]{1,0:T(8,128)} %collective-permute-done.part_ref, f32[192,768]{1,0:T(8,128)S(1)} %fusion.30.lift_ref, f32[24,768]{1,0:T(8,128)S(1)} %fusion.53.pick_ref), custom_call_target="tpu_custom_call" | custom-call | flops 15360000000 | bytes 4718592 | tf_op jit(solution)/shard_map/pallas_call | solution.py:263
  190.1 0.1 neg.16
  190.2 0.1 collective-permute-start.1
  190.3 0.1 pad.18.clone
  190.3 2.1 collective-permute-done.1
  192.5 5.4 %fusion.18 = f32[432,768]{1,0:T(8,128)S(1)} fusion(f32[768,768]{1,0:T(8,128)} %copy-done, f32[216,768]{1,0:T(8,128)S(1)} %neg.16, f32[216,768]{1,0:T(8,128)} %collective-permute-done.1), kind=kOutput, calls=%fused_computation.47 | convolution fusion | flops 3057979392 | bytes 5013504 | tf_op jit(solution)/shard_map/dot_general | solution.py:17
  197.9 0.1 slice_add_fusion
  198.0 1.2 pad_maximum_fusion.3
  199.2 2.3 maximum_maximum_fusion
  201.6 4.5 %fusion.11 = f32[456,1536]{1,0:T(8,128)S(1)} fusion(f32[384,6144]{1,0:T(8,128)} %all-gather.2.cloned.1.call-done, f32[456,768]{1,0:T(8,128)} %pad_maximum_fusion.3), kind=kOutput, calls=%fused_computation.36 | convolution fusion | flops 1613758464 | bytes 5861376 | tf_op jit(solution)/shard_map/dot_general | solution.py:17
  206.0 0.0 copy-start.7
  206.0 4.4 %fusion.14 = f32[456,1536]{1,0:T(8,128)S(1)} fusion(f32[384,6144]{1,0:T(8,128)} %all-gather.2.cloned.1.call-done, f32[456,768]{1,0:T(8,128)} %pad_maximum_fusion.3), kind=kOutput, calls=%fused_computation.39 | convolution fusion | flops 1613758464 | bytes 5861376 | tf_op jit(solution)/shard_map/dot_general | solution.py:17
  210.5 2.8 %convolution_add_fusion = f32[456,1536]{1,0:T(8,128)S(1)} fusion(f32[456,1536]{1,0:T(8,128)S(1)} %fusion.11, f32[384,6144]{1,0:T(8,128)S(1)} %copy-done.6, f32[456,768]{1,0:T(8,128)S(1)} %copy-done.7), kind=kOutput, calls=%fused_computation.5 | convolution fusion | flops 1614458880 | bytes 8663040 | tf_op jit(solution)/shard_map/dot_general | solution.py:17
  213.3 2.5 %convolution_add_fusion.1 = f32[456,1536]{1,0:T(8,128)S(1)} fusion(f32[456,1536]{1,0:T(8,128)S(1)} %fusion.14, f32[384,6144]{1,0:T(8,128)S(1)} %copy-done.6, f32[456,768]{1,0:T(8,128)S(1)} %copy-done.7), kind=kOutput, calls=%fused_computation.6 | convolution fusion | flops 1614458880 | bytes 8663040 | tf_op jit(solution)/shard_map/dot_general | solution.py:17
  215.9 1.9 pad_maximum_fusion.1
  217.8 0.5 copy-done.4
  218.2 0.1 collective-permute-start.2
  218.4 0.0 copy-start.26
  218.4 1.0 constant_dynamic-update-slice_fusion.19
  219.3 1.5 constant_dynamic-update-slice_fusion.18
  220.8 0.8 constant_dynamic-update-slice_fusion.17
  221.6 0.9 slice_dynamic-update-slice_fusion.1
  222.5 0.8 constant_dynamic-update-slice_fusion.16
  223.3 1.5 constant_dynamic-update-slice_fusion.15
  224.8 0.8 constant_dynamic-update-slice_fusion.14
  225.5 0.9 slice_dynamic-update-slice_fusion
  226.4 0.0 collective-permute-done.2
  226.5 0.0 copy-done.9
  226.5 0.0 copy-done.11
  226.5 0.0 copy-done.13
  226.5 0.0 copy-done.15
  226.5 0.0 copy-done.17
  226.6 5.1 %slice_select_fusion.1 = (f32[192,3072]{1,0:T(8,128)S(1)}, f32[192,3072]{1,0:T(8,128)S(1)}) fusion(f32[216,3072]{1,0:T(8,128)} %collective-permute-done.2, pred[]{:T(512)S(6)} %eq.18, f32[24,2304]{1,0:T(8,128)S(1)} %copy-done.17, f32[24,2304]{1,0:T(8,128)S(1)} %copy-done.19, f32[24,2304]{1,0:T(8,128)S(1)} %copy-done.13, ...), kind=kLoop, calls=%fused_computation.44 | loop fusion | flops 40108032 | bytes 15335425 | tf_op jit(solution)/shard_map/jit(_where)/select_n | solution.py:374
  231.7 2.0 slice_select_fusion
  233.7 2.7 %pad_maximum_fusion = f32[192,6144]{1,0:T(8,128)} fusion(f32[192,3072]{1,0:T(8,128)S(1)} %slice_select_fusion, f32[192,3072]{1,0:T(8,128)S(1)} %get-tuple-element.9), kind=kLoop, calls=%fused_computation | loop fusion | flops 1179648 | bytes 9437184 | tf_op jit(solution)/shard_map/concatenate | solution.py:376
  236.4 0.3 copy-done.3
  236.7 1.3 copy-done.5
  238.0 1.0 slice_select_fusion.3
  239.0 1.0 slice_select_fusion.2
  240.0 0.9 maximum_bitcast_fusion
  (63 shorter events, 0.4 us)
Async XLA Ops:
  7.2 194.4 %all-gather.2.cloned.1.call-start = ((), (), s32[]{:S(2)}) async-start(), calls=%async_computation | async-start | bytes 10027008 | tf_op jit(solution)/shard_map/all_gather | solution.py:294
  10.1 113.2 %copy-start.8 = (f32[24,2304]{1,0:T(8,128)}, f32[24,2304]{1,0:T(8,128)S(1)}, u32[]{:S(2)}) copy-start(f32[24,2304]{1,0:T(8,128)S(1)} %get-tuple-element.21) | copy-start | bytes 663556
  10.1 113.2 %copy-start.10 = (f32[24,2304]{1,0:T(8,128)}, f32[24,2304]{1,0:T(8,128)S(1)}, u32[]{:S(2)}) copy-start(f32[24,2304]{1,0:T(8,128)S(1)} %get-tuple-element.22) | copy-start | bytes 663556
  10.1 1.1 copy-start.28
  10.3 0.8 copy-start.24
  70.2 43.0 %copy-start.1 = (f32[16,24,2304]{2,1,0:T(8,128)}, f32[16,24,2304]{2,1,0:T(8,128)S(1)}, u32[]{:S(2)}) copy-start(f32[16,24,2304]{2,1,0:T(8,128)S(1)} %shard_map.49) | copy-start | bytes 10616836
  113.2 1.4 copy-start
  114.6 13.3 %collective-permute-start = (f32[768,768]{1,0:T(8,128)}, f32[768,768]{1,0:T(8,128)}, u32[]{:S(2)}, u32[]{:S(2)}) collective-permute-start(f32[768,768]{1,0:T(8,128)} %get-tuple-element.6.own_ref), channel_id=1, source_target_pairs={{0,16},{16,0},{1,17},{17,1},{2,18},{18,2},{3,19},{19,3},{4,20},{20... | collective-permute-start | bytes 7077896 | tf_op jit(solution)/shard_map/ppermute | solution.py:291
  120.6 1.9 copy-start.20
  120.6 2.7 %copy-start.12 = (f32[24,2304]{1,0:T(8,128)S(1)}, f32[24,2304]{1,0:T(8,128)}, u32[]{:S(2)}) copy-start(f32[24,2304]{1,0:T(8,128)} %get-tuple-element.24) | copy-start | bytes 663556
  120.6 2.7 %copy-start.14 = (f32[24,2304]{1,0:T(8,128)S(1)}, f32[24,2304]{1,0:T(8,128)}, u32[]{:S(2)}) copy-start(f32[24,2304]{1,0:T(8,128)} %get-tuple-element.26) | copy-start | bytes 663556
  120.7 2.7 %copy-start.16 = (f32[24,2304]{1,0:T(8,128)S(1)}, f32[24,2304]{1,0:T(8,128)}, u32[]{:S(2)}) copy-start(f32[24,2304]{1,0:T(8,128)} %get-tuple-element.29) | copy-start | bytes 663556
  120.7 2.7 %copy-start.18 = (f32[24,2304]{1,0:T(8,128)S(1)}, f32[24,2304]{1,0:T(8,128)}, u32[]{:S(2)}) copy-start(f32[24,2304]{1,0:T(8,128)} %get-tuple-element.30) | copy-start | bytes 663556
  122.5 0.7 copy-start.22
  190.2 2.3 collective-permute-start.1
  192.5 5.4 %copy-start.21 = (f32[96,768]{1,0:T(8,128)S(1)}, f32[96,768]{1,0:T(8,128)}, u32[]{:S(2)}) copy-start(f32[96,768]{1,0:T(8,128)} %copy-done.20) | copy-start | bytes 884740
  192.5 5.5 %copy-start.23 = (f32[96,768]{1,0:T(8,128)S(1)}, f32[96,768]{1,0:T(8,128)}, u32[]{:S(2)}) copy-start(f32[96,768]{1,0:T(8,128)} %copy-done.22) | copy-start | bytes 884740
  201.6 8.9 %copy-start.6 = (f32[384,6144]{1,0:T(8,128)S(1)}, f32[384,6144]{1,0:T(8,128)}, u32[]{:S(2)}) copy-start(f32[384,6144]{1,0:T(8,128)} %all-gather.2.cloned.1.call-done) | copy-start | bytes 28311556
  206.0 4.4 %copy-start.7 = (f32[456,768]{1,0:T(8,128)S(1)}, f32[456,768]{1,0:T(8,128)}, u32[]{:S(2)}) copy-start(f32[456,768]{1,0:T(8,128)} %maximum_maximum_fusion) | copy-start | bytes 4202500
  213.3 2.6 %copy-start.2 = (f32[456,1536]{1,0:T(8,128)}, f32[456,1536]{1,0:T(8,128)S(1)}, u32[]{:S(2)}) copy-start(f32[456,1536]{1,0:T(8,128)S(1)} %convolution_add_fusion) | copy-start | bytes 8404996
  215.8 2.4 copy-start.4
  218.2 8.3 %copy-start.9 = (f32[24,2304]{1,0:T(8,128)S(1)}, f32[24,2304]{1,0:T(8,128)}, u32[]{:S(2)}) copy-start(f32[24,2304]{1,0:T(8,128)} %copy-done.8) | copy-start | bytes 663556
  218.2 8.3 %copy-start.11 = (f32[24,2304]{1,0:T(8,128)S(1)}, f32[24,2304]{1,0:T(8,128)}, u32[]{:S(2)}) copy-start(f32[24,2304]{1,0:T(8,128)} %copy-done.10) | copy-start | bytes 663556
  218.2 8.3 %copy-start.13 = (f32[24,2304]{1,0:T(8,128)S(1)}, f32[24,2304]{1,0:T(8,128)}, u32[]{:S(2)}) copy-start(f32[24,2304]{1,0:T(8,128)} %get-tuple-element.24) | copy-start | bytes 663556
  218.2 8.2 %collective-permute-start.2 = (f32[216,3072]{1,0:T(8,128)}, f32[216,3072]{1,0:T(8,128)}, u32[]{:S(2)}, u32[]{:S(2)}) collective-permute-start(f32[216,3072]{1,0:T(8,128)} %pad_maximum_fusion.1), channel_id=1, source_target_pairs={{0,16},{16,0},{1,17},{17,1},{2,18},{18,2},{3,19},{19,3},{4,20},{20... | collective-permute-start | bytes 7962632 | tf_op jit(solution)/shard_map/ppermute | solution.py:291
  218.4 8.1 %copy-start.15 = (f32[24,2304]{1,0:T(8,128)S(1)}, f32[24,2304]{1,0:T(8,128)}, u32[]{:S(2)}) copy-start(f32[24,2304]{1,0:T(8,128)} %get-tuple-element.26) | copy-start | bytes 663556
  218.4 8.2 %copy-start.17 = (f32[24,2304]{1,0:T(8,128)S(1)}, f32[24,2304]{1,0:T(8,128)}, u32[]{:S(2)}) copy-start(f32[24,2304]{1,0:T(8,128)} %get-tuple-element.29) | copy-start | bytes 663556
  218.4 8.2 %copy-start.19 = (f32[24,2304]{1,0:T(8,128)S(1)}, f32[24,2304]{1,0:T(8,128)}, u32[]{:S(2)}) copy-start(f32[24,2304]{1,0:T(8,128)} %get-tuple-element.30) | copy-start | bytes 663556
  218.4 8.2 %copy-start.25 = (f32[96,384]{1,0:T(8,128)S(1)}, f32[96,384]{1,0:T(8,128)}, u32[]{:S(2)}) copy-start(f32[96,384]{1,0:T(8,128)} %get-tuple-element.14) | copy-start | bytes 442372
  218.4 8.2 %copy-start.26 = (f32[96,384]{1,0:T(8,128)S(1)}, f32[96,384]{1,0:T(8,128)}, u32[]{:S(2)}) copy-start(f32[96,384]{1,0:T(8,128)} %get-tuple-element.41) | copy-start | bytes 442372
  226.4 5.3 %copy-start.27 = (f32[24,3840]{1,0:T(8,128)}, f32[24,3840]{1,0:T(8,128)S(1)}, u32[]{:S(2)}) copy-start(f32[24,3840]{1,0:T(8,128)S(1)} %slice_dynamic-update-slice_fusion) | copy-start | bytes 1105924
  233.7 3.0 %copy-start.3 = (f32[456,1536]{1,0:T(8,128)S(1)}, f32[456,1536]{1,0:T(8,128)}, u32[]{:S(2)}) copy-start(f32[456,1536]{1,0:T(8,128)} %copy-done.2) | copy-start | bytes 8404996
  233.7 4.3 %copy-start.5 = (f32[456,1536]{1,0:T(8,128)S(1)}, f32[456,1536]{1,0:T(8,128)}, u32[]{:S(2)}) copy-start(f32[456,1536]{1,0:T(8,128)} %copy-done.4) | copy-start | bytes 8404996
Sparse Core Ops, SparseCore 0:
  11.3 135.8 all-gather.1
where the time goes:
time: 250 us; the launch traced here: 248 us
  Pallas kernels  164 us (66%)
  matrix products  29.6 us (12%)
  other arithmetic  23.7 us (9%)
  between operations  14.7 us (6%)
  local copies, waits for them, and re-layouts  8.93 us (4%)
  starting transfers between devices  4.63 us (2%)
    pallas_call x2, Pallas kernels, call(): pl.pallas_call(kernel, out_shape=[jax.ShapeDtypeStruct(o, jnp.float32) fo...  105 us
    pallas_call x1, Pallas kernels, quick_gather(): pl.pallas_call(functools.partial(gather_kernel, n, bits, chunks), out_sha...  58.9 us
    dot_general x11, matrix products, dot(): jnp.dot(left, right, precision=precision, preferred_element_type=jnp.floa...  29.6 us
    unnamed x67, local copies, waits for them, and re-layouts  7.72 us
    select_n x1, other arithmetic, body(): left = jnp.where(first, own_map, cross[:2 * n])  5.12 us
  transfers between devices with their start and end apart: 4, of which 1 were waited for; matrix products, arithmetic and copies ran while one was open for 10% of the time, Pallas kernels for 66%

commit v1 on v0

--- a/solution.py
+++ b/solution.py
@@ -11,6 +11,7 @@
 HIGH = lax.Precision.HIGH
 BLOCK = 128
 GROUP = 4
+MESH = pl.DeviceIdType.MESH
 
 
 def dot(left, right, precision=HIGHEST):
@@ -23,50 +24,51 @@
     )
 
 
+def invert_step(blk, lane, g, carry):
+    size = blk.shape[0]
+    k = g * GROUP
+    full = blk[...]
+    cols = [
+        jnp.take_along_axis(full, jnp.full((size, size), k + i, jnp.int32), axis=1)
+        for i in range(GROUP)
+    ]
+    rows = [blk[pl.ds(k + i, 1), :] for i in range(GROUP)]
+    wide = [jnp.broadcast_to(r, (8, size)) for r in rows]
+    pivots = [
+        [
+            jnp.take_along_axis(wide[i], jnp.full((8, size), k + j, jnp.int32), axis=1)
+            for j in range(GROUP)
+        ]
+        for i in range(GROUP)
+    ]
+    inside = (lane >= k) & (lane < k + GROUP)
+    wide = [
+        jnp.where(lane == k + i, 1.0, jnp.where(inside, 0.0, wide[i])) for i in range(GROUP)
+    ]
+    for i in range(GROUP):
+        p = 1.0 / pivots[i][i]
+        wide[i] = wide[i] * p
+        for j in range(i + 1, GROUP):
+            pivots[i][j] = pivots[i][j] * p
+        for l in range(GROUP):
+            if l != i:
+                f = pivots[l][i]
+                wide[l] = wide[l] - f * wide[i]
+                for j in range(i + 1, GROUP):
+                    pivots[l][j] = pivots[l][j] - f * pivots[i][j]
+    result = jnp.where(inside, 0.0, full)
+    for i in range(GROUP):
+        result = result - cols[i] * wide[i][0:1]
+    blk[...] = result
+    for i in range(GROUP):
+        blk[pl.ds(k + i, 1), :] = wide[i][0:1]
+    return carry
+
+
 def invert_block(blk):
     size = blk.shape[0]
     lane = lax.broadcasted_iota(jnp.int32, (1, size), 1)
-
-    def step(g, carry):
-        k = g * GROUP
-        full = blk[...]
-        cols = [
-            jnp.take_along_axis(full, jnp.full((size, size), k + i, jnp.int32), axis=1)
-            for i in range(GROUP)
-        ]
-        rows = [blk[pl.ds(k + i, 1), :] for i in range(GROUP)]
-        wide = [jnp.broadcast_to(r, (8, size)) for r in rows]
-        pivots = [
-            [
-                jnp.take_along_axis(wide[i], jnp.full((8, size), k + j, jnp.int32), axis=1)
-                for j in range(GROUP)
-            ]
-            for i in range(GROUP)
-        ]
-        inside = (lane >= k) & (lane < k + GROUP)
-        wide = [
-            jnp.where(lane == k + i, 1.0, jnp.where(inside, 0.0, wide[i])) for i in range(GROUP)
-        ]
-        for i in range(GROUP):
-            p = 1.0 / pivots[i][i]
-            wide[i] = wide[i] * p
-            for j in range(i + 1, GROUP):
-                pivots[i][j] = pivots[i][j] * p
-            for l in range(GROUP):
-                if l != i:
-                    f = pivots[l][i]
-                    wide[l] = wide[l] - f * wide[i]
-                    for j in range(i + 1, GROUP):
-                        pivots[l][j] = pivots[l][j] - f * pivots[i][j]
-        result = jnp.where(inside, 0.0, full)
-        for i in range(GROUP):
-            result = result - cols[i] * wide[i][0:1]
-        blk[...] = result
-        for i in range(GROUP):
-            blk[pl.ds(k + i, 1), :] = wide[i][0:1]
-        return carry
-
-    lax.fori_loop(0, size // GROUP, step, 0)
+    lax.fori_loop(0, size // GROUP, functools.partial(invert_step, blk, lane), 0)
 
 
 def invert(mat, blk, col):
@@ -277,7 +279,7 @@
     )(*args)
 
 
-def body(dtn, interface_perm):
+def plain_body(dtn, interface_perm):
     a, b = dtn[0], dtn[1]
     count = a.shape[1]
     f = a.shape[2] // 6
@@ -390,7 +392,529 @@
     return (solution_first[None], second[None], merged_map)
 
 
+def split3(x):
+    high = x.astype(jnp.bfloat16)
+    rest = x - high.astype(jnp.float32)
+    mid = rest.astype(jnp.bfloat16)
+    low = (rest - mid.astype(jnp.float32)).astype(jnp.bfloat16)
+    return high, mid, low
+
+
+def dims(left, right):
+    return (((left,), (right,)), ((), ()))
+
+
+def bdot(left, right, dn):
+    return lax.dot_general(left, right, dn, preferred_element_type=jnp.float32)
+
+
+def pick_left(onehot, x, contract=1):
+    return sum(bdot(onehot, part, dims(contract, 0)) for part in split3(x))
+
+
+def pick_right(x, onehot, contract=0):
+    return sum(bdot(part, onehot, dims(1, contract)) for part in split3(x))
+
+
+def xdot(left, right, dn):
+    return lax.dot_general(left, right, dn, precision=HIGHEST, preferred_element_type=jnp.float32)
+
+
+def split2(x):
+    high = x.astype(jnp.bfloat16)
+    low = (x - high.astype(jnp.float32)).astype(jnp.bfloat16)
+    return high, low
+
+
+def dot3(left, right, dn):
+    a, b = left
+    c, d = right
+    return bdot(a, c, dn) + (bdot(a, d, dn) + bdot(b, c, dn))
+
+
+NN = dims(1, 0)
+NT = dims(1, 1)
+TN = dims(0, 0)
+
+
+def invert_small(mat, blk, col, tick):
+    order = mat.shape[0]
+    count = order // BLOCK
+    eye = (
+        lax.broadcasted_iota(jnp.int32, (BLOCK, BLOCK), 0)
+        == lax.broadcasted_iota(jnp.int32, (BLOCK, BLOCK), 1)
+    ).astype(jnp.float32)
+    for j in range(count):
+        here = pl.ds(j * BLOCK, BLOCK)
+        blk[...] = mat[here, here]
+        invert_steps(blk, tick)
+        col[...] = mat[:, here]
+        mat[:, here] = jnp.zeros((order, BLOCK), jnp.float32)
+        mat[here, here] = eye
+        mat[here, :] = xdot(blk[...], mat[here, :], NN)
+        for i in range(count):
+            if i != j:
+                there = pl.ds(i * BLOCK, BLOCK)
+                mat[there, :] = mat[there, :] - xdot(col[there, :], mat[here, :], NN)
+        tick()
+
+
+def invert_steps(blk, tick, parts=2):
+    size = blk.shape[0]
+    lane = lax.broadcasted_iota(jnp.int32, (1, size), 1)
+    total = size // GROUP
+    for part in range(parts):
+        lax.fori_loop(
+            part * total // parts,
+            (part + 1) * total // parts,
+            functools.partial(invert_step, blk, lane),
+            0,
+        )
+        if part + 1 < parts:
+            tick()
+
+
+class Gather:
+    def __init__(self, ref, lead, block, cols, order, me, n, sends, recvs):
+        self.ref, self.lead, self.block, self.cols, self.order = ref, lead, block, cols, order
+        self.me, self.n, self.sends, self.recvs = me, n, sends, recvs
+
+    def view(self, stage, arrived):
+        m = self.n.bit_length() - 1
+        index = []
+        for b in range(m - 1, -1, -1):
+            bit = 1 << b
+            own = (self.me // bit) % 2
+            if bit in self.order[:stage]:
+                index.append(slice(None))
+            elif arrived and bit == self.order[stage]:
+                index.append(1 - own)
+            else:
+                index.append(own)
+        blocks = pl.ds(self.block[0], self.block[1] - self.block[0])
+        cols = pl.ds(self.cols[0], self.cols[1] - self.cols[0])
+        return self.ref.at[(*self.lead, blocks, *index, slice(None), cols)]
+
+    def copy(self, stage):
+        piece = self.view(stage, False)
+        return pltpu.make_async_remote_copy(
+            src_ref=piece,
+            dst_ref=piece,
+            send_sem=self.sends.at[stage],
+            recv_sem=self.recvs.at[stage],
+            device_id={"row": flip(self.me, self.order[stage])},
+            device_id_type=MESH,
+        )
+
+
+def merge_kernel(
+    plan, perm_ref, dtn_ref, z_ref, lift_ref, own_ref, y_ref, gx_ref, bulk_ref,
+    small, mat1, mat2, mat3, tee, blk, col, edge, ss, part, rhs, hold,
+    fill_sem, send0, recv0, send1, recv1, send2, recv2, core_send, core_recv, swap_send, swap_recv,
+):
+    n, f, count = plan["n"], plan["f"], plan["count"]
+    bits = plan["bits"]
+    me = lax.axis_index("row")
+    pair = lax.axis_index("box")
+    half = lax.rem(pair, 2)
+    other = pair + 1 - 2 * half
+    yface, free = 3 - half, 2 + half
+    spot = [(me // bit) % 2 for bit in bits]
+
+    def at(face):
+        return pl.ds(face * f, f) if isinstance(face, int) else pl.ds(pl.multiple_of(face * f, BLOCK), f)
+
+    narrow = [(0, 1, 1), (1, 0, 0), (0, 1, yface), (1, 0, yface), (0, yface, yface), (1, yface, yface)]
+    outer = [(0, free, 4, 5), (1, free, 4, 5)]
+    wide = [(h, 1 - h, c) for h in range(2) for c in outer[h]]
+    wide += [(h, yface, c) for h in range(2) for c in outer[h]]
+    fills = []
+    for b, (h, r, c) in enumerate(narrow):
+        fills.append(
+            pltpu.make_async_copy(dtn_ref.at[h, r, :, at(c)], small.at[(b, *spot)], fill_sem.at[b])
+        )
+    for b, (h, r, c) in enumerate(wide):
+        fills.append(
+            pltpu.make_async_copy(
+                dtn_ref.at[h, r, :, at(c)], bulk_ref.at[(0, b, *spot)], fill_sem.at[len(narrow) + b]
+            )
+        )
+    for one in fills:
+        one.start()
+
+    barrier = pltpu.get_barrier_semaphore()
+    for bit in bits:
+        pl.semaphore_signal(barrier, inc=1, device_id={"row": flip(me, bit)}, device_id_type=MESH)
+    pl.semaphore_signal(barrier, inc=1, device_id={"box": other}, device_id_type=MESH)
+    pl.semaphore_wait(barrier, len(bits) + 1)
+
+    def gathers(ref, lead, chunks, sends, recvs):
+        return [
+            Gather(ref, lead, block, cols, order, me, n, sends.at[i], recvs.at[i])
+            for i, (block, cols, order) in enumerate(chunks)
+        ]
+
+    first = gathers(small, (), plan["first"], send0, recv0)
+    rest = gathers(small, (), plan["rest"], send1, recv1)
+    bulk = gathers(bulk_ref, (0,), plan["bulk"], send2, recv2)
+    last = len(bits)
+
+    def cross(i, stage):
+        g = bulk[i]
+        view = g.view(0, False) if stage < 0 else g.view(stage, True)
+        there = Gather(bulk_ref, (1,), g.block, g.cols, g.order, me, n, None, None)
+        target = there.view(0, False) if stage < 0 else there.view(stage, True)
+        return pltpu.make_async_remote_copy(
+            src_ref=view,
+            dst_ref=target,
+            send_sem=core_send.at[i, stage + 1],
+            recv_sem=core_recv.at[i, stage + 1],
+            device_id={"box": other},
+            device_id_type=MESH,
+        )
+
+    def advance(group, i, stage):
+        g = group[i]
+        if stage > 0:
+            g.copy(stage - 1).wait_recv()
+        if stage < last:
+            g.copy(stage).start()
+        if group is bulk:
+            cross(i, stage - 1).start()
+
+    events = list(plan["events"])
+
+    def tick():
+        if events:
+            for name, i, stage in events.pop(0):
+                advance({"first": first, "rest": rest, "bulk": bulk}[name], i, stage)
+
+    for one in fills[: len(narrow)]:
+        one.wait()
+    for stage in range(last + 1):
+        for i in range(len(first)):
+            advance(first, i, stage)
+        if stage == last - 1:
+            for i in range(len(rest)):
+                advance(rest, i, 0)
+    for one in fills[len(narrow) :]:
+        one.wait()
+
+    def block(b):
+        return small[b].reshape(f, f)
+
+    count_f = f // BLOCK
+    whole = (perm_ref[...] == lax.broadcasted_iota(jnp.int32, (f, f), 1)).astype(jnp.bfloat16)
+    hold[...] = pick_left(whole, block(1))
+    mat1[...] = block(0) + pick_right(hold[...], whole, 1)
+    tick()
+    invert_small(mat1, blk, col, tick)
+
+    edge[:, :f] = block(2)
+    edge[:, f:] = pick_left(whole, block(3))
+
+    def rows_of(i):
+        return pl.ds(pl.multiple_of(i * BLOCK, BLOCK), BLOCK)
+
+    @pl.loop(0, count_f)
+    def _(i):
+        gx_ref[0, 0, rows_of(i), :] = xdot(mat1[rows_of(i), :], edge[...], NN)
+
+    tick()
+
+    def swap(b):
+        return pltpu.make_async_remote_copy(
+            src_ref=ss.at[b],
+            dst_ref=part.at[b],
+            send_sem=swap_send.at[b],
+            recv_sem=swap_recv.at[b],
+            device_id={"box": other},
+            device_id_type=MESH,
+        )
+
+    for b, (i, j, y) in enumerate([(0, 0, 4), (0, 1, None), (1, 1, 5)]):
+
+        @pl.loop(0, count_f)
+        def _(k):
+            left = edge[:, pl.ds(pl.multiple_of(i * f + k * BLOCK, BLOCK), BLOCK)]
+            value = -xdot(left, gx_ref[0, 0, :, j * f : (j + 1) * f], TN)
+            ss[b, rows_of(k), :] = value
+
+        if y is not None:
+            ss[b] = ss[b] + block(y)
+        if b > 0:
+            swap(b - 1).start()
+    tick()
+
+    outers = []
+    for h in range(2):
+        outers.append(
+            jnp.concatenate([dtn_ref[h, r, :, pl.ds((1 - h) * f, f)] for r in outer[h]], axis=0)
+        )
+    swap(2).start()
+    m = 4 * count
+    joined = jnp.concatenate([outers[0], pick_right(outers[1], whole, 1)], axis=0)
+    value = -xdot(joined, mat1[...], NN)
+    lift_ref[:, :f] = value
+    lift_ref[:, f:] = pick_right(value, whole)
+    own_at = pl.ds(pl.multiple_of(me * count, 8), count)
+    mine = mat1[own_at, :]
+    own_ref[:, :f] = -mine
+    own_ref[:, f:] = -pick_right(mine, whole)
+    y_ref[...] = -gx_ref[0, 0, own_at, :]
+    rhs[: 2 * m, :] = -xdot(joined, gx_ref[0, 0], NN)
+    for h in range(2):
+        side = jnp.concatenate([dtn_ref[h, r, :, at(yface)] for r in outer[h]], axis=0)
+        rhs[h * m : (h + 1) * m, h * f : (h + 1) * f] += side
+    rhs[2 * m :, :] = (
+        lax.broadcasted_iota(jnp.int32, (count, 2 * f), 1)
+        == half * f + me * count + lax.broadcasted_iota(jnp.int32, (count, 2 * f), 0)
+    ).astype(jnp.float32)
+
+    @pl.loop(0, count_f)
+    def _(i):
+        picked = whole_cols(perm_ref, i, f)
+        gx_ref[0, 1, rows_of(i), :] = pick_left(picked, gx_ref[0, 0], 0)
+
+    tick()
+    swap(0).wait_recv()
+    mat2[...] = ss[0] + part[0]
+    invert_small(mat2, blk, col, tick)
+    gx_copy = pltpu.make_async_remote_copy(
+        src_ref=gx_ref.at[0],
+        dst_ref=gx_ref.at[1],
+        send_sem=swap_send.at[3],
+        recv_sem=swap_recv.at[3],
+        device_id={"box": other},
+        device_id_type=MESH,
+    )
+    gx_copy.start()
+    swap(1).wait_recv()
+    hold[...] = ss[1] + part[1]
+
+    @pl.loop(0, count_f)
+    def _(i):
+        tee[rows_of(i), :] = xdot(mat2[rows_of(i), :], hold[...], NN)
+
+    swap(2).wait_recv()
+
+    @pl.loop(0, count_f)
+    def _(i):
+        mat3[rows_of(i), :] = (
+            ss[2, rows_of(i), :]
+            + part[2, rows_of(i), :]
+            - xdot(hold[:, rows_of(i)], tee[...], TN)
+        )
+
+    tick()
+    invert_small(mat3, blk, col, tick)
+    left = rhs[:, :f]
+    second = xdot(xdot(left, tee[...], NN) - rhs[:, f:], mat3[...], NN)
+    z_ref[:, f:] = second
+    z_ref[:, :f] = -xdot(left, mat2[...], NN) - xdot(second, tee[...], NT)
+    while events:
+        tick()
+    for b in range(3):
+        swap(b).wait_send()
+    gx_copy.wait()
+    for group in (first, rest, bulk):
+        for g in group:
+            for stage in range(last):
+                g.copy(stage).wait_send()
+    for i in range(len(bulk)):
+        for stage in range(-1, last):
+            cross(i, stage).wait()
+
+
+def whole_cols(perm_ref, i, f):
+    return (
+        perm_ref[...] == lax.broadcasted_iota(jnp.int32, (f, BLOCK), 1) + i * BLOCK
+    ).astype(jnp.bfloat16)
+
+
+def product_kernel(
+    half_ref, z_ref, lift_ref, own_ref, y_ref, gx_ref, dtn_ref, one_ref, two_ref,
+    first_ref, second_ref, map_ref, high, low,
+):
+    step = pl.program_id(0)
+    q, h, c = step // 8, (step // 4) % 2, step % 4
+    half = half_ref[0]
+    rows, f = z_ref.shape[0], z_ref.shape[1] // 2
+    count = own_ref.shape[0]
+    m = 4 * count
+
+    @pl.when(step % 8 == 0)
+    def _():
+        z = split2(z_ref[...])
+        for k in range(2):
+            value = -dot3(z, split2(gx_ref[0, k]), NT)
+
+            a, b = split2(value)
+            high[k, :rows, :], low[k, :rows, :] = a, b
+
+            @pl.when(q == 0)
+            def _():
+                a, b = split2(value[: 2 * m] + lift_ref[:, k * f : (k + 1) * f])
+                high[k, : 2 * m, :], low[k, : 2 * m, :] = a, b
+
+            a, b = split2(own_ref[:, k * f : (k + 1) * f])
+            high[k, rows:, :], low[k, rows:, :] = a, b
+
+    @pl.when(step == 0)
+    def _():
+        for k in range(2):
+            at = pl.multiple_of((5 * k + 2 - half) * f, BLOCK)
+            first_ref[:, pl.ds(at, f)] = y_ref[:, k * f : (k + 1) * f]
+
+    res = dot3((high[h], low[h]), split2(one_ref[0, 0]), NN)
+    zs = split2(z_ref[:, pl.ds(pl.multiple_of(h * f, BLOCK), f)])
+    add = dot3(zs, split2(two_ref[0, 0]), NN)
+    map_ref[...] = (res[: 2 * m] + add[: 2 * m]).reshape(map_ref.shape)
+    second_ref[...] = res[2 * m : rows] + add[2 * m :]
+
+    @pl.when(q == 0)
+    def _():
+        where = 5 * h + jnp.where(c == 0, 0, jnp.where(c == 1, 1 + half, c + 1))
+        first_ref[:, pl.ds(pl.multiple_of(where * f, BLOCK), f)] = res[rows:]
+        face = jnp.where(c == 0, h, jnp.where(c == 1, 2 + half, c + 2))
+        cols = pl.ds(pl.multiple_of(face * f, BLOCK), f)
+        for k, r in enumerate((h, 2 + half, 4, 5)):
+            map_ref[4 * h + k] += dtn_ref[h, r, :, cols]
+
+
+def fast_body(dtn, interface_perm):
+    _, faces, count, width = dtn.shape
+    f = width // faces
+    n = lax.axis_size("row")
+    bits = []
+    bit = n // 2
+    while bit:
+        bits.append(bit)
+        bit //= 2
+    near, far = bits[-2:], bits[:-2]
+    orders = [far + near, far + near[::-1], near[::-1] + far]
+    tiles = f // BLOCK
+    cuts = [(BLOCK * (tiles * i // 3), BLOCK * (tiles * (i + 1) // 3)) for i in range(3)]
+    spans = [(0, 6, 0), (6, 12, 1), (12, 16, 2)]
+    last = len(bits)
+    plan = {
+        "n": n,
+        "f": f,
+        "count": count,
+        "bits": bits,
+        "first": [((0, 2), cut, order) for cut, order in zip(cuts, orders)],
+        "rest": [((2, 6), cut, order) for cut, order in zip(cuts, orders)],
+        "bulk": [((a, b), (0, f), orders[k]) for a, b, k in spans],
+        "events": [],
+    }
+    nb = len(plan["bulk"])
+    rest = [[("rest", i, s) for i in range(3)] for s in range(1, last + 1)]
+    bulk = [[("bulk", i, s) for i in range(nb)] for s in range(last + 1)]
+    when = {0: rest[0], 2: rest[1] + bulk[0], 4: rest[2], 6: rest[3] + bulk[1], 11: bulk[2], 16: bulk[3]}
+    plan["events"] = [when.get(k, []) for k in range(24)] + bulk[4:]
+    split = (2,) * last
+    vmem = pl.BlockSpec(memory_space=pltpu.VMEM)
+    dma = pltpu.SemaphoreType.DMA
+    rows = 9 * count
+    f32 = jnp.float32
+    z, lift, own, y, gx, bulk_all = pl.pallas_call(
+        functools.partial(merge_kernel, plan),
+        out_shape=[
+            jax.ShapeDtypeStruct(s, f32)
+            for s in (
+                (rows, 2 * f),
+                (8 * count, 2 * f),
+                (count, 2 * f),
+                (count, 2 * f),
+                (2, 2, f, 2 * f),
+                (2, 16, *split, count, f),
+            )
+        ],
+        in_specs=[vmem, vmem],
+        out_specs=[vmem] * 5 + [pl.BlockSpec(memory_space=pl.ANY)],
+        scratch_shapes=[
+            pltpu.VMEM((6, *split, count, f), f32),
+            pltpu.VMEM((f, f), f32),
+            pltpu.VMEM((f, f), f32),
+            pltpu.VMEM((f, f), f32),
+            pltpu.VMEM((f, f), f32),
+            pltpu.VMEM((BLOCK, BLOCK), f32),
+            pltpu.VMEM((f, BLOCK), f32),
+            pltpu.VMEM((f, 2 * f), f32),
+            pltpu.VMEM((3, f, f), f32),
+            pltpu.VMEM((3, f, f), f32),
+            pltpu.VMEM((rows, 2 * f), f32),
+            pltpu.VMEM((f, f), f32),
+            dma((22,)),
+            dma((3, last)),
+            dma((3, last)),
+            dma((3, last)),
+            dma((3, last)),
+            dma((nb, last)),
+            dma((nb, last)),
+            dma((nb, last + 1)),
+            dma((nb, last + 1)),
+            dma((4,)),
+            dma((4,)),
+        ],
+        compiler_params=pltpu.CompilerParams(
+            collective_id=0, has_side_effects=True, vmem_limit_bytes=48 * 1024 * 1024
+        ),
+    )(interface_perm[0][:, None], dtn)
+    bulk_all = bulk_all.reshape(2, 16, f, f)
+    half = (lax.axis_index("box") % 2).astype(jnp.int32)
+    lane = 2 * f
+
+    def fixed(shape):
+        return pl.BlockSpec(shape, lambda s, r: (0,) * len(shape))
+
+    def column(s, r):
+        own_half = r[0]
+        return jnp.where(s < 8, own_half, 1 - own_half) * 8 + s % 8
+
+    first, second, merged = pl.pallas_call(
+        product_kernel,
+        grid_spec=pltpu.PrefetchScalarGridSpec(
+            num_scalar_prefetch=1,
+            grid=(16,),
+            in_specs=[
+                fixed((rows, lane)),
+                fixed((8 * count, lane)),
+                fixed((count, lane)),
+                fixed((count, lane)),
+                pl.BlockSpec((1, 2, f, lane), lambda s, r: (s // 8, 0, 0, 0)),
+                fixed(dtn.shape),
+                pl.BlockSpec((1, 1, f, f), lambda s, r: (s // 8, s % 8, 0, 0)),
+                pl.BlockSpec((1, 1, f, f), lambda s, r: (s // 8, 8 + s % 8, 0, 0)),
+            ],
+            out_specs=[
+                fixed((count, 10 * f)),
+                pl.BlockSpec((count, f), lambda s, r: (0, column(s, r))),
+                pl.BlockSpec((8, count, f), lambda s, r: (0, 0, column(s, r))),
+            ],
+            scratch_shapes=[
+                pltpu.VMEM((2, rows + count, f), jnp.bfloat16),
+                pltpu.VMEM((2, rows + count, f), jnp.bfloat16),
+            ],
+        ),
+        out_shape=[
+            jax.ShapeDtypeStruct((count, 10 * f), f32),
+            jax.ShapeDtypeStruct((count, 16 * f), f32),
+            jax.ShapeDtypeStruct((8, count, 16 * f), f32),
+        ],
+        compiler_params=pltpu.CompilerParams(vmem_limit_bytes=40 * 1024 * 1024),
+    )(half[None], z, lift, own, y, gx, dtn, bulk_all, bulk_all)
+    return (first[None], second[None], merged[None])
+
+
 def solution(mesh):
+    def body(dtn, interface_perm):
+        n = mesh.shape["row"]
+        count = dtn.shape[2]
+        if count % 8 == 0 and n >= 8 and n & (n - 1) == 0:
+            return fast_body(dtn, interface_perm)
+        return plain_body(dtn, interface_perm)
+
     return jax.shard_map(
         body,
         mesh=mesh,

time: 250 us -> 179 us (0.72)
  matrix products: 29.6 us -> 0 us
  other arithmetic: 23.7 us -> 0 us
  between operations: 14.7 us -> 0.73 us
  Pallas kernels: 164 us -> 170 us
  starting transfers between devices: 4.63 us -> 0 us
    dot_general x11 -> x0, matrix products: 29.6 us -> none  [dot(): jnp.dot(left, right, precision=precision, preferred_element_type=jnp.floa...]
    select_n x7 -> x0, other arithmetic: 9.92 us -> none  [the longest x1 5.12 us: body(): left = jnp.where(first, own_map, cross[:2 * n])]
    concatenate x4 -> x0, other arithmetic: 6.3 us -> none  [the longest x1 2.72 us: body(): jnp.concatenate([left, right], axis=1).reshape(1, 8, count, 4 * w)]
    pallas_call x3 -> x2, Pallas kernels: 164 us -> 170 us  [the longest x1 146 us: fast_body(): pl.pallas_call(functools.partial(merge_kernel, plan), out_shape=[jax.Shap...]
    ppermute x3 -> x0, starting transfers between devices: 4.59 us -> none  [swap(): return lax.ppermute(x, 'box', [(i, i ^ 1) for i in range(n)])]
    squeeze x1 -> x0, other arithmetic: 2.85 us -> none  [body(): a[0]]
    unnamed x67 -> x6, local copies, waits for them, and re-layouts: 7.72 us -> 5.83 us
  transfers between devices with their start and end apart: 4 -> 0, of which waited for: 1 -> 0; matrix products, arithmetic and copies ran while one was open for 10% -> 0% of each run, Pallas kernels for 66% -> 0%
where the time goes in v1:
time: 179 us; the launch traced here: 177 us
  Pallas kernels  170 us (95%)
  local copies, waits for them, and re-layouts  6.64 us (4%)
    pallas_call x1, Pallas kernels, fast_body(): pl.pallas_call(functools.partial(merge_kernel, plan), out_shape=[jax.Shap...  146 us
    pallas_call x1, Pallas kernels, fast_body(): pl.pallas_call(product_kernel, grid_spec=pltpu.PrefetchScalarGridSpec(num...  23.5 us
    unnamed x6, local copies, waits for them, and re-layouts  5.83 us

profile of v1, /device:TPU:15, one launch (start us, length us, event | category | flops | bytes accessed | tf_op | source)
XLA Modules:
  0.0 177.1 jit_solution(10505588582893819888)
XLA Ops:
  0.6 0.8 copy.5.perm_ref
  1.5 0.0 copy-start
  1.5 1.7 copy-done
  3.2 146.3 %shard_map.49 = (f32[216,768]{1,0:T(8,128)S(1)}, f32[192,768]{1,0:T(8,128)S(1)}, f32[24,768]{1,0:T(8,128)S(1)}, f32[24,768]{1,0:T(8,128)S(1)}, f32[2,2,384,768]{...) custom-call(s32[384,1]{1,0:T(8,128)S(1)} %copy.5.perm_ref, f32[2,6,24,2304]{3,2,1,0:T(8,128)S(1)} %copy-done), custom_call_target="tpu_custom_call" | custom-call | tf_op jit(solution)/shard_map/pallas_call | solution.py:820
  149.5 0.0 copy-start.1
  149.5 1.7 copy-done.1
  151.3 0.0 copy-start.2
  151.3 2.3 %copy-done.2 = f32[2,2,384,768]{3,2,1,0:T(8,128)S(1)} copy-done((f32[2,2,384,768]{3,2,1,0:T(8,128)S(1)}, f32[2,2,384,768]{3,2,1,0:T(8,128)}, u32[]{:S(2)}) %copy-start.2) | copy-done | bytes 4718616
  153.6 23.5 %shard_map.50 = (f32[24,3840]{1,0:T(8,128)}, f32[24,6144]{1,0:T(8,128)}, f32[8,24,6144]{2,1,0:T(8,128)}) custom-call(s32[1]{0:T(128)} %bitcast.half_ref, f32[216,768]{1,0:T(8,128)S(1)} %get-tuple-element.12.z_ref, f32[192,768]{1,0:T(8,128)S(1)} %get-tuple-element.13.lift_ref, f32[24,768]{1,0:T(8,128)S(1)} %get-tuple-element.14.own_ref, ...), custom_call_target="tpu_custom_call" | custom-call | tf_op jit(solution)/shard_map/pallas_call | solution.py:875
Async XLA Ops:
  1.5 1.8 copy-start
  149.5 1.8 copy-start.1
  151.3 2.3 %copy-start.2 = (f32[2,2,384,768]{3,2,1,0:T(8,128)S(1)}, f32[2,2,384,768]{3,2,1,0:T(8,128)}, u32[]{:S(2)}) copy-start(f32[2,2,384,768]{3,2,1,0:T(8,128)} %get-tuple-element.16.gx_ref) | copy-start | bytes 14155780

commit v2 on v1

--- a/solution.py
+++ b/solution.py
@@ -437,6 +437,14 @@
 TN = dims(0, 0)
 
 
+FIRST = ['xyba', 'byax', 'baxy', 'byxa', 'abyx', 'bxay']
+FIRST_EVENTS = [(0, 0), (1, 0), (4, 0), (2, 0), (3, 0), (0, 1), (5, 0), (1, 1), (4, 1), (2, 1), (3, 1), (5, 1), (0, 2), (4, 2), (2, 2), (1, 2), (3, 2), (5, 2), (4, 3), (0, 3), (2, 3), (1, 3), (3, 3), (5, 3)]
+REST = ['bayx', 'bxay', 'aybx', 'bayx', 'abxy', 'baxy']
+BULK = [((0, 1), 'axby'), ((1, 2), 'bayx'), ((2, 3), 'xbay'), ((3, 4), 'yabx'), ((4, 6), 'axby'), ((6, 8), 'bayx'), ((8, 10), 'ybxa'), ((10, 12), 'bxay'), ((12, 14), 'byxa'), ((14, 16), 'bayx')]
+BULK_START = 3
+EVENTS = [(1, 0, 0), (1, 2, 0), (1, 1, 0), (1, 4, 0), (2, 3, 0), (3, 5, 0), (3, 1, 1), (3, 2, 1), (3, 0, 1), (4, 4, 1), (4, 3, 1), (4, 8, 0), (5, 0, 2), (5, 1, 2), (5, 9, 0), (7, 12, 0), (7, 5, 1), (7, 4, 2), (8, 6, 0), (8, 3, 2), (8, 2, 2), (8, 7, 0), (9, 10, 0), (9, 0, 3), (10, 1, 3), (10, 5, 2), (11, 11, 0), (11, 9, 1), (12, 4, 3), (12, 13, 0), (12, 7, 1), (12, 2, 3), (13, 14, 0), (13, 5, 3), (14, 3, 3), (14, 6, 1), (14, 15, 0), (14, 11, 1), (14, 7, 2), (15, 10, 1), (15, 8, 1), (15, 14, 1), (16, 13, 1), (18, 15, 1), (18, 12, 1), (18, 11, 2), (19, 7, 3), (21, 8, 2), (21, 9, 2), (23, 15, 2), (23, 14, 2), (25, 6, 2), (26, 8, 3), (28, 13, 2), (29, 6, 3), (29, 11, 3), (31, 10, 2), (32, 12, 2), (36, 9, 3), (36, 14, 3), (36, 13, 3), (41, 15, 3), (41, 12, 3), (41, 10, 3)]
+
+
 def invert_small(mat, blk, col, tick):
     order = mat.shape[0]
     count = order // BLOCK
@@ -459,7 +467,7 @@
         tick()
 
 
-def invert_steps(blk, tick, parts=2):
+def invert_steps(blk, tick, parts=4):
     size = blk.shape[0]
     lane = lax.broadcasted_iota(jnp.int32, (1, size), 1)
     total = size // GROUP
@@ -526,8 +534,7 @@
 
     narrow = [(0, 1, 1), (1, 0, 0), (0, 1, yface), (1, 0, yface), (0, yface, yface), (1, yface, yface)]
     outer = [(0, free, 4, 5), (1, free, 4, 5)]
-    wide = [(h, 1 - h, c) for h in range(2) for c in outer[h]]
-    wide += [(h, yface, c) for h in range(2) for c in outer[h]]
+    wide = [(h, r, c) for h in range(2) for c in outer[h] for r in (1 - h, yface)]
     fills = []
     for b, (h, r, c) in enumerate(narrow):
         fills.append(
@@ -583,20 +590,22 @@
             cross(i, stage - 1).start()
 
     events = list(plan["events"])
+    groups = {"first": first, "rest": rest, "bulk": bulk}
 
     def tick():
         if events:
             for name, i, stage in events.pop(0):
-                advance({"first": first, "rest": rest, "bulk": bulk}[name], i, stage)
+                advance(groups[name], i, stage)
 
     for one in fills[: len(narrow)]:
         one.wait()
-    for stage in range(last + 1):
-        for i in range(len(first)):
-            advance(first, i, stage)
-        if stage == last - 1:
-            for i in range(len(rest)):
-                advance(rest, i, 0)
+    for i in range(len(first)):
+        advance(first, i, 0)
+    for i, stage in plan["first_events"]:
+        advance(first, i, stage + 1)
+        if (i, stage) == plan["first_events"][-len(first)]:
+            for k in range(len(rest)):
+                advance(rest, k, 0)
     for one in fills[len(narrow) :]:
         one.wait()
 
@@ -632,7 +641,7 @@
             device_id_type=MESH,
         )
 
-    for b, (i, j, y) in enumerate([(0, 0, 4), (0, 1, None), (1, 1, 5)]):
+    for b, (i, j) in enumerate([(0, 0), (0, 1), (1, 1)]):
 
         @pl.loop(0, count_f)
         def _(k):
@@ -640,11 +649,11 @@
             value = -xdot(left, gx_ref[0, 0, :, j * f : (j + 1) * f], TN)
             ss[b, rows_of(k), :] = value
 
-        if y is not None:
-            ss[b] = ss[b] + block(y)
-        if b > 0:
-            swap(b - 1).start()
     tick()
+    ss[0] = ss[0] + block(4)
+    swap(1).start()
+    ss[2] = ss[2] + block(5)
+    swap(0).start()
 
     outers = []
     for h in range(2):
@@ -733,32 +742,33 @@
 
 
 def product_kernel(
-    half_ref, z_ref, lift_ref, own_ref, y_ref, gx_ref, dtn_ref, one_ref, two_ref,
+    half_ref, z_ref, lift_ref, own_ref, y_ref, gx_ref, dtn_ref, wide_ref,
     first_ref, second_ref, map_ref, high, low,
 ):
     step = pl.program_id(0)
-    q, h, c = step // 8, (step // 4) % 2, step % 4
+    q, h, c = step // 4, (step // 2) % 2, 2 * (step % 2)
     half = half_ref[0]
     rows, f = z_ref.shape[0], z_ref.shape[1] // 2
     count = own_ref.shape[0]
     m = 4 * count
 
-    @pl.when(step % 8 == 0)
+    @pl.when(step % 4 == 0)
     def _():
         z = split2(z_ref[...])
         for k in range(2):
+            high[k, :rows, f:], low[k, :rows, f:] = [one[:, k * f : (k + 1) * f] for one in z]
+            zero = jnp.zeros((count, f), jnp.bfloat16)
+            high[k, rows:, f:], low[k, rows:, f:] = zero, zero
             value = -dot3(z, split2(gx_ref[0, k]), NT)
-
-            a, b = split2(value)
-            high[k, :rows, :], low[k, :rows, :] = a, b
+            high[k, :rows, :f], low[k, :rows, :f] = split2(value)
 
             @pl.when(q == 0)
             def _():
                 a, b = split2(value[: 2 * m] + lift_ref[:, k * f : (k + 1) * f])
-                high[k, : 2 * m, :], low[k, : 2 * m, :] = a, b
+                high[k, : 2 * m, :f], low[k, : 2 * m, :f] = a, b
 
             a, b = split2(own_ref[:, k * f : (k + 1) * f])
-            high[k, rows:, :], low[k, rows:, :] = a, b
+            high[k, rows:, :f], low[k, rows:, :f] = a, b
 
     @pl.when(step == 0)
     def _():
@@ -766,20 +776,25 @@
             at = pl.multiple_of((5 * k + 2 - half) * f, BLOCK)
             first_ref[:, pl.ds(at, f)] = y_ref[:, k * f : (k + 1) * f]
 
-    res = dot3((high[h], low[h]), split2(one_ref[0, 0]), NN)
-    zs = split2(z_ref[:, pl.ds(pl.multiple_of(h * f, BLOCK), f)])
-    add = dot3(zs, split2(two_ref[0, 0]), NN)
-    map_ref[...] = (res[: 2 * m] + add[: 2 * m]).reshape(map_ref.shape)
-    second_ref[...] = res[2 * m : rows] + add[2 * m :]
+    def columns(k):
+        return wide_ref[0, 2 * k : 2 * k + 2].reshape(2 * f, f)
+
+    right = split2(jnp.concatenate([columns(0), columns(1)], axis=1))
+    res = dot3((high[h], low[h]), right, NN)
+    map_ref[...] = res[: 2 * m].reshape(map_ref.shape)
+    second_ref[...] = res[2 * m : rows]
 
     @pl.when(q == 0)
     def _():
-        where = 5 * h + jnp.where(c == 0, 0, jnp.where(c == 1, 1 + half, c + 1))
-        first_ref[:, pl.ds(pl.multiple_of(where * f, BLOCK), f)] = res[rows:]
-        face = jnp.where(c == 0, h, jnp.where(c == 1, 2 + half, c + 2))
-        cols = pl.ds(pl.multiple_of(face * f, BLOCK), f)
-        for k, r in enumerate((h, 2 + half, 4, 5)):
-            map_ref[4 * h + k] += dtn_ref[h, r, :, cols]
+        for k in range(2):
+            place = c + k
+            here = slice(k * f, (k + 1) * f)
+            where = 5 * h + jnp.where(place == 0, 0, jnp.where(place == 1, 1 + half, place + 1))
+            first_ref[:, pl.ds(pl.multiple_of(where * f, BLOCK), f)] = res[rows:, here]
+            face = jnp.where(place == 0, h, jnp.where(place == 1, 2 + half, place + 2))
+            cols = pl.ds(pl.multiple_of(face * f, BLOCK), f)
+            for i, r in enumerate((h, 2 + half, 4, 5)):
+                map_ref[4 * h + i, :, here] += dtn_ref[h, r, :, cols]
 
 
 def fast_body(dtn, interface_perm):
@@ -791,27 +806,35 @@
     while bit:
         bits.append(bit)
         bit //= 2
-    near, far = bits[-2:], bits[:-2]
-    orders = [far + near, far + near[::-1], near[::-1] + far]
+    last = len(bits)
     tiles = f // BLOCK
     cuts = [(BLOCK * (tiles * i // 3), BLOCK * (tiles * (i + 1) // 3)) for i in range(3)]
-    spans = [(0, 6, 0), (6, 12, 1), (12, 16, 2)]
-    last = len(bits)
+    named = dict(zip("bayx", bits))
+
+    def order(letters):
+        return [named[one] for one in letters]
+
+    six = [((a, a + 1), cut) for a in range(2) for cut in cuts]
+    rest_parts = [((a, a + 2), cut) for a in (2, 4) for cut in cuts]
+    events = [[] for _ in range(1 + max(k for k, _, _ in EVENTS))]
+    events[BULK_START] = [("bulk", i, 0) for i in range(len(BULK))]
+    for k, i, stage in EVENTS:
+        if i < len(REST):
+            events[k].append(("rest", i, stage + 1))
+        else:
+            events[k].append(("bulk", i - len(REST), stage + 1))
+    nb = len(BULK)
     plan = {
         "n": n,
         "f": f,
         "count": count,
         "bits": bits,
-        "first": [((0, 2), cut, order) for cut, order in zip(cuts, orders)],
-        "rest": [((2, 6), cut, order) for cut, order in zip(cuts, orders)],
-        "bulk": [((a, b), (0, f), orders[k]) for a, b, k in spans],
-        "events": [],
+        "first": [(*part, order(o)) for part, o in zip(six, FIRST)],
+        "first_events": FIRST_EVENTS,
+        "rest": [(*part, order(o)) for part, o in zip(rest_parts, REST)],
+        "bulk": [(blocks, (0, f), order(o)) for blocks, o in BULK],
+        "events": events,
     }
-    nb = len(plan["bulk"])
-    rest = [[("rest", i, s) for i in range(3)] for s in range(1, last + 1)]
-    bulk = [[("bulk", i, s) for i in range(nb)] for s in range(last + 1)]
-    when = {0: rest[0], 2: rest[1] + bulk[0], 4: rest[2], 6: rest[3] + bulk[1], 11: bulk[2], 16: bulk[3]}
-    plan["events"] = [when.get(k, []) for k in range(24)] + bulk[4:]
     split = (2,) * last
     vmem = pl.BlockSpec(memory_space=pltpu.VMEM)
     dma = pltpu.SemaphoreType.DMA
@@ -846,10 +869,10 @@
             pltpu.VMEM((rows, 2 * f), f32),
             pltpu.VMEM((f, f), f32),
             dma((22,)),
-            dma((3, last)),
-            dma((3, last)),
-            dma((3, last)),
-            dma((3, last)),
+            dma((6, last)),
+            dma((6, last)),
+            dma((6, last)),
+            dma((6, last)),
             dma((nb, last)),
             dma((nb, last)),
             dma((nb, last + 1)),
@@ -870,31 +893,30 @@
 
     def column(s, r):
         own_half = r[0]
-        return jnp.where(s < 8, own_half, 1 - own_half) * 8 + s % 8
+        return jnp.where(s < 4, own_half, 1 - own_half) * 4 + s % 4
 
     first, second, merged = pl.pallas_call(
         product_kernel,
         grid_spec=pltpu.PrefetchScalarGridSpec(
             num_scalar_prefetch=1,
-            grid=(16,),
+            grid=(8,),
             in_specs=[
                 fixed((rows, lane)),
                 fixed((8 * count, lane)),
                 fixed((count, lane)),
                 fixed((count, lane)),
-                pl.BlockSpec((1, 2, f, lane), lambda s, r: (s // 8, 0, 0, 0)),
+                pl.BlockSpec((1, 2, f, lane), lambda s, r: (s // 4, 0, 0, 0)),
                 fixed(dtn.shape),
-                pl.BlockSpec((1, 1, f, f), lambda s, r: (s // 8, s % 8, 0, 0)),
-                pl.BlockSpec((1, 1, f, f), lambda s, r: (s // 8, 8 + s % 8, 0, 0)),
+                pl.BlockSpec((1, 4, f, f), lambda s, r: (s // 4, s % 4, 0, 0)),
             ],
             out_specs=[
                 fixed((count, 10 * f)),
-                pl.BlockSpec((count, f), lambda s, r: (0, column(s, r))),
-                pl.BlockSpec((8, count, f), lambda s, r: (0, 0, column(s, r))),
+                pl.BlockSpec((count, lane), lambda s, r: (0, column(s, r))),
+                pl.BlockSpec((8, count, lane), lambda s, r: (0, 0, column(s, r))),
             ],
             scratch_shapes=[
-                pltpu.VMEM((2, rows + count, f), jnp.bfloat16),
-                pltpu.VMEM((2, rows + count, f), jnp.bfloat16),
+                pltpu.VMEM((2, rows + count, 2 * f), jnp.bfloat16),
+                pltpu.VMEM((2, rows + count, 2 * f), jnp.bfloat16),
             ],
         ),
         out_shape=[
@@ -903,7 +925,7 @@
             jax.ShapeDtypeStruct((8, count, 16 * f), f32),
         ],
         compiler_params=pltpu.CompilerParams(vmem_limit_bytes=40 * 1024 * 1024),
-    )(half[None], z, lift, own, y, gx, dtn, bulk_all, bulk_all)
+    )(half[None], z, lift, own, y, gx, dtn, bulk_all)
     return (first[None], second[None], merged[None])
 
 
@@ -911,7 +933,7 @@
     def body(dtn, interface_perm):
         n = mesh.shape["row"]
         count = dtn.shape[2]
-        if count % 8 == 0 and n >= 8 and n & (n - 1) == 0:
+        if count % 8 == 0 and n == 1 << len(FIRST[0]):
             return fast_body(dtn, interface_perm)
         return plain_body(dtn, interface_perm)
 

time: 179 us -> 160 us (0.89)
  Pallas kernels: 170 us -> 151 us
    pallas_call x1, Pallas kernels: 146 us -> 134 us  [fast_body(): pl.pallas_call(functools.partial(merge_kernel, plan), out_shape=[jax.Shap...]
    pallas_call x1, Pallas kernels: 23.5 us -> 17.5 us  [fast_body(): pl.pallas_call(product_kernel, grid_spec=pltpu.PrefetchScalarGridSpec(num...]
where the time goes in v2:
time: 160 us; the launch traced here: 159 us
  Pallas kernels  151 us (94%)
  local copies, waits for them, and re-layouts  6.64 us (4%)
    pallas_call x1, Pallas kernels, fast_body(): pl.pallas_call(functools.partial(merge_kernel, plan), out_shape=[jax.Shap...  134 us
    pallas_call x1, Pallas kernels, fast_body(): pl.pallas_call(product_kernel, grid_spec=pltpu.PrefetchScalarGridSpec(num...  17.5 us
    unnamed x6, local copies, waits for them, and re-layouts  5.83 us

profile of v2, /device:TPU:15, one launch (start us, length us, event | category | flops | bytes accessed | tf_op | source)
XLA Modules:
  0.0 158.5 jit_solution(13752171254753113653)
XLA Ops:
  0.6 0.8 copy.5.perm_ref
  1.5 0.0 copy-start
  1.5 1.7 %copy-done = f32[2,6,24,2304]{3,2,1,0:T(8,128)S(1)} copy-done((f32[2,6,24,2304]{3,2,1,0:T(8,128)S(1)}, f32[2,6,24,2304]{3,2,1,0:T(8,128)}, u32[]{:S(2)}) %copy-start) | copy-done | bytes 2654232
  3.2 133.7 %shard_map.49 = (f32[216,768]{1,0:T(8,128)S(1)}, f32[192,768]{1,0:T(8,128)S(1)}, f32[24,768]{1,0:T(8,128)S(1)}, f32[24,768]{1,0:T(8,128)S(1)}, f32[2,2,384,768]{...) custom-call(s32[384,1]{1,0:T(8,128)S(1)} %copy.5.perm_ref, f32[2,6,24,2304]{3,2,1,0:T(8,128)S(1)} %copy-done), custom_call_target="tpu_custom_call" | custom-call | tf_op jit(solution)/shard_map/pallas_call | solution.py:843
  136.9 0.0 copy-start.1
  136.9 1.7 %copy-done.1 = f32[2,6,24,2304]{3,2,1,0:T(8,128)S(1)} copy-done((f32[2,6,24,2304]{3,2,1,0:T(8,128)S(1)}, f32[2,6,24,2304]{3,2,1,0:T(8,128)}, u32[]{:S(2)}) %copy-start.1) | copy-done | bytes 2654232
  138.7 0.0 copy-start.2
  138.7 2.3 %copy-done.2 = f32[2,2,384,768]{3,2,1,0:T(8,128)S(1)} copy-done((f32[2,2,384,768]{3,2,1,0:T(8,128)S(1)}, f32[2,2,384,768]{3,2,1,0:T(8,128)}, u32[]{:S(2)}) %copy-start.2) | copy-done | bytes 4718616
  141.0 17.5 %shard_map.50 = (f32[24,3840]{1,0:T(8,128)}, f32[24,6144]{1,0:T(8,128)}, f32[8,24,6144]{2,1,0:T(8,128)}) custom-call(s32[1]{0:T(128)} %bitcast.half_ref, f32[216,768]{1,0:T(8,128)S(1)} %get-tuple-element.12.z_ref, f32[192,768]{1,0:T(8,128)S(1)} %get-tuple-element.13.lift_ref, f32[24,768]{1,0:T(8,128)S(1)} %get-tuple-element.14.own_ref, ...), custom_call_target="tpu_custom_call" | custom-call | tf_op jit(solution)/shard_map/pallas_call | solution.py:898
Async XLA Ops:
  1.5 1.8 %copy-start = (f32[2,6,24,2304]{3,2,1,0:T(8,128)S(1)}, f32[2,6,24,2304]{3,2,1,0:T(8,128)}, u32[]{:S(2)}) copy-start(f32[2,6,24,2304]{3,2,1,0:T(8,128)} %dtn_ref.3) | copy-start | bytes 7962628
  136.9 1.8 %copy-start.1 = (f32[2,6,24,2304]{3,2,1,0:T(8,128)S(1)}, f32[2,6,24,2304]{3,2,1,0:T(8,128)}, u32[]{:S(2)}) copy-start(f32[2,6,24,2304]{3,2,1,0:T(8,128)} %dtn_ref.3) | copy-start | bytes 7962628
  138.7 2.3 %copy-start.2 = (f32[2,2,384,768]{3,2,1,0:T(8,128)S(1)}, f32[2,2,384,768]{3,2,1,0:T(8,128)}, u32[]{:S(2)}) copy-start(f32[2,2,384,768]{3,2,1,0:T(8,128)} %get-tuple-element.16.gx_ref) | copy-start | bytes 14155780

commit v3 on v2

--- a/solution.py
+++ b/solution.py
@@ -439,10 +439,109 @@
 
 FIRST = ['xyba', 'byax', 'baxy', 'byxa', 'abyx', 'bxay']
 FIRST_EVENTS = [(0, 0), (1, 0), (4, 0), (2, 0), (3, 0), (0, 1), (5, 0), (1, 1), (4, 1), (2, 1), (3, 1), (5, 1), (0, 2), (4, 2), (2, 2), (1, 2), (3, 2), (5, 2), (4, 3), (0, 3), (2, 3), (1, 3), (3, 3), (5, 3)]
-REST = ['bayx', 'bxay', 'aybx', 'bayx', 'abxy', 'baxy']
-BULK = [((0, 1), 'axby'), ((1, 2), 'bayx'), ((2, 3), 'xbay'), ((3, 4), 'yabx'), ((4, 6), 'axby'), ((6, 8), 'bayx'), ((8, 10), 'ybxa'), ((10, 12), 'bxay'), ((12, 14), 'byxa'), ((14, 16), 'bayx')]
+REST = ['byxa', 'abyx', 'baxy', 'bayx', 'abxy', 'baxy']
+BULK = [((0, 1), 'ybxa'), ((1, 2), 'baxy'), ((2, 3), 'bayx'), ((3, 4), 'baxy'), ((4, 6), 'byax'), ((6, 8), 'bxay'), ((8, 10), 'bxya'), ((10, 12), 'abxy'), ((12, 14), 'bayx'), ((14, 16), 'ybxa')]
 BULK_START = 3
-EVENTS = [(1, 0, 0), (1, 2, 0), (1, 1, 0), (1, 4, 0), (2, 3, 0), (3, 5, 0), (3, 1, 1), (3, 2, 1), (3, 0, 1), (4, 4, 1), (4, 3, 1), (4, 8, 0), (5, 0, 2), (5, 1, 2), (5, 9, 0), (7, 12, 0), (7, 5, 1), (7, 4, 2), (8, 6, 0), (8, 3, 2), (8, 2, 2), (8, 7, 0), (9, 10, 0), (9, 0, 3), (10, 1, 3), (10, 5, 2), (11, 11, 0), (11, 9, 1), (12, 4, 3), (12, 13, 0), (12, 7, 1), (12, 2, 3), (13, 14, 0), (13, 5, 3), (14, 3, 3), (14, 6, 1), (14, 15, 0), (14, 11, 1), (14, 7, 2), (15, 10, 1), (15, 8, 1), (15, 14, 1), (16, 13, 1), (18, 15, 1), (18, 12, 1), (18, 11, 2), (19, 7, 3), (21, 8, 2), (21, 9, 2), (23, 15, 2), (23, 14, 2), (25, 6, 2), (26, 8, 3), (28, 13, 2), (29, 6, 3), (29, 11, 3), (31, 10, 2), (32, 12, 2), (36, 9, 3), (36, 14, 3), (36, 13, 3), (41, 15, 3), (41, 12, 3), (41, 10, 3)]
+EVENTS = [(1, 0, 0), (1, 1, 0), (1, 2, 0), (1, 4, 0), (2, 3, 0), (3, 5, 0), (3, 0, 1), (4, 2, 1), (4, 1, 1), (4, 6, 0), (5, 3, 1), (5, 4, 1), (5, 0, 2), (5, 15, 0), (6, 5, 1), (7, 7, 0), (7, 1, 2), (7, 2, 2), (8, 8, 0), (8, 13, 0), (8, 3, 2), (8, 4, 2), (8, 9, 0), (9, 5, 2), (10, 10, 0), (11, 2, 3), (12, 1, 3), (12, 11, 0), (12, 0, 3), (13, 4, 3), (13, 12, 0), (13, 3, 3), (13, 7, 1), (14, 5, 3), (14, 14, 0), (14, 11, 1), (14, 8, 1), (15, 10, 1), (15, 6, 1), (15, 7, 2), (15, 9, 1), (15, 8, 2), (16, 12, 1), (18, 15, 1), (19, 6, 2), (20, 7, 3), (22, 13, 1), (22, 11, 2), (22, 8, 3), (23, 14, 1), (24, 9, 2), (24, 12, 2), (27, 10, 2), (27, 15, 2), (31, 6, 3), (31, 11, 3), (31, 13, 2), (35, 14, 2), (38, 12, 3), (38, 9, 3), (38, 10, 3), (41, 15, 3), (41, 13, 3), (41, 14, 3)]
+
+
+def inv2(a, b, c):
+    ra = 1.0 / a
+    t = b * ra
+    rs = 1.0 / (c - b * t)
+    u = t * rs
+    return ra + t * u, -u, rs
+
+
+def inv4(d):
+    a0, a1, a2 = inv2(d[0][0], d[0][1], d[1][1])
+    t = [
+        [a0 * d[0][2] + a1 * d[1][2], a0 * d[0][3] + a1 * d[1][3]],
+        [a1 * d[0][2] + a2 * d[1][2], a1 * d[0][3] + a2 * d[1][3]],
+    ]
+    s0, s1, s2 = inv2(
+        d[2][2] - (d[0][2] * t[0][0] + d[1][2] * t[1][0]),
+        d[2][3] - (d[0][2] * t[0][1] + d[1][2] * t[1][1]),
+        d[3][3] - (d[0][3] * t[0][1] + d[1][3] * t[1][1]),
+    )
+    u = [[t[i][0] * s0 + t[i][1] * s1, t[i][0] * s1 + t[i][1] * s2] for i in range(2)]
+    e00 = a0 + (u[0][0] * t[0][0] + u[0][1] * t[0][1])
+    e01 = a1 + (u[0][0] * t[1][0] + u[0][1] * t[1][1])
+    e11 = a2 + (u[1][0] * t[1][0] + u[1][1] * t[1][1])
+    return [
+        [e00, e01, -u[0][0], -u[0][1]],
+        [e01, e11, -u[1][0], -u[1][1]],
+        [-u[0][0], -u[1][0], s0, s1],
+        [-u[0][1], -u[1][1], s1, s2],
+    ]
+
+
+def spread(x, lane_index):
+    return jnp.take_along_axis(x, jnp.full(x.shape, lane_index, jnp.int32), axis=1)
+
+
+def row(x, i):
+    return jnp.broadcast_to(x[i : i + 1], x.shape)
+
+
+def weigh(weights, values):
+    return (weights[0] * values[0] + weights[1] * values[1]) + (weights[2] * values[2] + weights[3] * values[3])
+
+
+def diag(tile, first, sub):
+    e = [spread(tile, first + j) for j in range(4)]
+    return [[row(e[j], sub + i) if j >= i else None for j in range(4)] for i in range(4)]
+
+
+def flat(d):
+    return tuple(d[i][j] for i in range(4) for j in range(i, 4))
+
+
+def unflat(c):
+    it = iter(c)
+    d = [[None] * 4 for _ in range(4)]
+    for i in range(4):
+        for j in range(i, 4):
+            d[i][j] = next(it)
+    return d
+
+
+def pivot_step(blk, lane, k, sub, d):
+    size = blk.shape[0]
+    inside = (lane >= k) & (lane < k + 4)
+    start = pl.multiple_of(jnp.minimum(k + 4 - (4 - sub) % 8, size - 8), 8)
+    skip = (sub + 4) % 8
+    g = inv4(d)
+    own = blk[pl.ds(pl.multiple_of(k - sub, 8), 8), :]
+    near = own if sub == 0 else blk[pl.ds(start, 8), :]
+    rows = [jnp.where(lane == k + i, 1.0, jnp.where(inside, 0.0, row(own, sub + i))) for i in range(4)]
+    w = [weigh(g[i], rows) for i in range(4)]
+    nearc = [spread(near, k + i) for i in range(4)]
+    new = jnp.where(inside, 0.0, near) - weigh(nearc, w)
+    nd = diag(new, lax.rem(k + 4, size), skip)
+    full = blk[...]
+    wide = jnp.broadcast_to(inside[0:1], full.shape)
+    cols = [jnp.take_along_axis(full, jnp.full(full.shape, k + i, jnp.int32), axis=1) for i in range(4)]
+    result = jnp.where(wide, 0.0, full)
+    for i in range(4):
+        result = result - cols[i] * w[i][0:1]
+    blk[...] = result
+    for i in range(4):
+        blk[pl.ds(k + i, 1), :] = w[i][0:1]
+    return nd
+
+
+def pivots_begin(blk):
+    return flat(diag(blk[0:8, :], 0, 0))
+
+
+def pivots_run(blk, start, stop, carry):
+    lane = lax.broadcasted_iota(jnp.int32, (8, blk.shape[1]), 1)
+    def body(t, c):
+        d = pivot_step(blk, lane, 8 * t, 0, unflat(c))
+        d = pivot_step(blk, lane, 8 * t + 4, 4, d)
+        return flat(d)
+    return lax.fori_loop(start, stop, body, carry)
 
 
 def invert_small(mat, blk, col, tick):
@@ -455,7 +554,12 @@
     for j in range(count):
         here = pl.ds(j * BLOCK, BLOCK)
         blk[...] = mat[here, here]
-        invert_steps(blk, tick)
+        carry = pivots_begin(blk)
+        total = BLOCK // 8
+        for part in range(4):
+            carry = pivots_run(blk, part * total // 4, (part + 1) * total // 4, carry)
+            if part < 3:
+                tick()
         col[...] = mat[:, here]
         mat[:, here] = jnp.zeros((order, BLOCK), jnp.float32)
         mat[here, here] = eye
@@ -465,21 +569,6 @@
                 there = pl.ds(i * BLOCK, BLOCK)
                 mat[there, :] = mat[there, :] - xdot(col[there, :], mat[here, :], NN)
         tick()
-
-
-def invert_steps(blk, tick, parts=4):
-    size = blk.shape[0]
-    lane = lax.broadcasted_iota(jnp.int32, (1, size), 1)
-    total = size // GROUP
-    for part in range(parts):
-        lax.fori_loop(
-            part * total // parts,
-            (part + 1) * total // parts,
-            functools.partial(invert_step, blk, lane),
-            0,
-        )
-        if part + 1 < parts:
-            tick()
 
 
 class Gather:

time: 160 us -> 148 us (0.925)
  Pallas kernels: 151 us -> 140 us
    pallas_call x1, Pallas kernels: 134 us -> 123 us  [fast_body(): pl.pallas_call(functools.partial(merge_kernel, plan), out_shape=[jax.Shap...]
where the time goes in v3:
time: 148 us
  Pallas kernels  140 us (95%)
  local copies, waits for them, and re-layouts  6.64 us (4%)
    pallas_call x1, Pallas kernels, fast_body(): pl.pallas_call(functools.partial(merge_kernel, plan), out_shape=[jax.Shap...  123 us
    pallas_call x1, Pallas kernels, fast_body(): pl.pallas_call(product_kernel, grid_spec=pltpu.PrefetchScalarGridSpec(num...  17.5 us
    unnamed x6, local copies, waits for them, and re-layouts  5.83 us

profile of v3, /device:TPU:15, one launch (start us, length us, event | category | flops | bytes accessed | tf_op | source)
XLA Modules:
  0.0 147.6 jit_solution(9524991614277730545)
XLA Ops:
  0.6 0.8 copy.5.perm_ref
  1.5 0.0 copy-start
  1.5 1.7 %copy-done = f32[2,6,24,2304]{3,2,1,0:T(8,128)S(1)} copy-done((f32[2,6,24,2304]{3,2,1,0:T(8,128)S(1)}, f32[2,6,24,2304]{3,2,1,0:T(8,128)}, u32[]{:S(2)}) %copy-start) | copy-done | bytes 2654232
  3.2 122.8 %shard_map.49 = (f32[216,768]{1,0:T(8,128)S(1)}, f32[192,768]{1,0:T(8,128)S(1)}, f32[24,768]{1,0:T(8,128)S(1)}, f32[24,768]{1,0:T(8,128)S(1)}, f32[2,2,384,768]{...) custom-call(s32[384,1]{1,0:T(8,128)S(1)} %copy.5.perm_ref, f32[2,6,24,2304]{3,2,1,0:T(8,128)S(1)} %copy-done), custom_call_target="tpu_custom_call" | custom-call | tf_op jit(solution)/shard_map/pallas_call | solution.py:932
  126.0 0.0 copy-start.1
  126.0 1.7 %copy-done.1 = f32[2,6,24,2304]{3,2,1,0:T(8,128)S(1)} copy-done((f32[2,6,24,2304]{3,2,1,0:T(8,128)S(1)}, f32[2,6,24,2304]{3,2,1,0:T(8,128)}, u32[]{:S(2)}) %copy-start.1) | copy-done | bytes 2654232
  127.8 0.0 copy-start.2
  127.8 2.3 %copy-done.2 = f32[2,2,384,768]{3,2,1,0:T(8,128)S(1)} copy-done((f32[2,2,384,768]{3,2,1,0:T(8,128)S(1)}, f32[2,2,384,768]{3,2,1,0:T(8,128)}, u32[]{:S(2)}) %copy-start.2) | copy-done | bytes 4718616
  130.1 17.5 %shard_map.50 = (f32[24,3840]{1,0:T(8,128)}, f32[24,6144]{1,0:T(8,128)}, f32[8,24,6144]{2,1,0:T(8,128)}) custom-call(s32[1]{0:T(128)} %bitcast.half_ref, f32[216,768]{1,0:T(8,128)S(1)} %get-tuple-element.12.z_ref, f32[192,768]{1,0:T(8,128)S(1)} %get-tuple-element.13.lift_ref, f32[24,768]{1,0:T(8,128)S(1)} %get-tuple-element.14.own_ref, ...), custom_call_target="tpu_custom_call" | custom-call | tf_op jit(solution)/shard_map/pallas_call | solution.py:987
Async XLA Ops:
  1.5 1.8 %copy-start = (f32[2,6,24,2304]{3,2,1,0:T(8,128)S(1)}, f32[2,6,24,2304]{3,2,1,0:T(8,128)}, u32[]{:S(2)}) copy-start(f32[2,6,24,2304]{3,2,1,0:T(8,128)} %dtn_ref.3) | copy-start | bytes 7962628
  126.0 1.8 %copy-start.1 = (f32[2,6,24,2304]{3,2,1,0:T(8,128)S(1)}, f32[2,6,24,2304]{3,2,1,0:T(8,128)}, u32[]{:S(2)}) copy-start(f32[2,6,24,2304]{3,2,1,0:T(8,128)} %dtn_ref.3) | copy-start | bytes 7962628
  127.8 2.3 %copy-start.2 = (f32[2,2,384,768]{3,2,1,0:T(8,128)S(1)}, f32[2,2,384,768]{3,2,1,0:T(8,128)}, u32[]{:S(2)}) copy-start(f32[2,2,384,768]{3,2,1,0:T(8,128)} %get-tuple-element.16.gx_ref) | copy-start | bytes 14155780

commit v4 on v3

--- a/solution.py
+++ b/solution.py
@@ -605,8 +605,8 @@
 
 
 def merge_kernel(
-    plan, perm_ref, dtn_ref, z_ref, lift_ref, own_ref, y_ref, gx_ref, bulk_ref,
-    small, mat1, mat2, mat3, tee, blk, col, edge, ss, part, rhs, hold,
+    plan, perm_ref, dtn_any, z_ref, lift_ref, own_ref, y_ref, gx_ref, bulk_ref,
+    small, mat1, mat2, mat3, tee, blk, col, edge, ss, part, rhs, hold, dtn_ref,
     fill_sem, send0, recv0, send1, recv1, send2, recv2, core_send, core_recv, swap_send, swap_recv,
 ):
     n, f, count = plan["n"], plan["f"], plan["count"]
@@ -627,7 +627,7 @@
     fills = []
     for b, (h, r, c) in enumerate(narrow):
         fills.append(
-            pltpu.make_async_copy(dtn_ref.at[h, r, :, at(c)], small.at[(b, *spot)], fill_sem.at[b])
+            pltpu.make_async_copy(dtn_any.at[h, r, :, at(c)], small.at[(b, *spot)], fill_sem.at[b])
         )
     for b, (h, r, c) in enumerate(wide):
         fills.append(
@@ -635,8 +635,10 @@
                 dtn_ref.at[h, r, :, at(c)], bulk_ref.at[(0, b, *spot)], fill_sem.at[len(narrow) + b]
             )
         )
-    for one in fills:
+    load = pltpu.make_async_copy(dtn_any, dtn_ref, fill_sem.at[len(narrow) + len(wide)])
+    for one in fills[: len(narrow)]:
         one.start()
+    load.start()
 
     barrier = pltpu.get_barrier_semaphore()
     for bit in bits:
@@ -695,6 +697,9 @@
         if (i, stage) == plan["first_events"][-len(first)]:
             for k in range(len(rest)):
                 advance(rest, k, 0)
+    load.wait()
+    for one in fills[len(narrow) :]:
+        one.start()
     for one in fills[len(narrow) :]:
         one.wait()
 
@@ -702,14 +707,14 @@
         return small[b].reshape(f, f)
 
     count_f = f // BLOCK
-    whole = (perm_ref[...] == lax.broadcasted_iota(jnp.int32, (f, f), 1)).astype(jnp.bfloat16)
-    hold[...] = pick_left(whole, block(1))
-    mat1[...] = block(0) + pick_right(hold[...], whole, 1)
+    whole = (perm_ref[...] == lax.broadcasted_iota(jnp.int32, (f, f), 0)).astype(jnp.bfloat16)
+    hold[...] = pick_left(whole, block(1), 0)
+    mat1[...] = block(0) + pick_right(hold[...], whole)
     tick()
     invert_small(mat1, blk, col, tick)
 
     edge[:, :f] = block(2)
-    edge[:, f:] = pick_left(whole, block(3))
+    edge[:, f:] = pick_left(whole, block(3), 0)
 
     def rows_of(i):
         return pl.ds(pl.multiple_of(i * BLOCK, BLOCK), BLOCK)
@@ -751,14 +756,14 @@
         )
     swap(2).start()
     m = 4 * count
-    joined = jnp.concatenate([outers[0], pick_right(outers[1], whole, 1)], axis=0)
+    joined = jnp.concatenate([outers[0], pick_right(outers[1], whole)], axis=0)
     value = -xdot(joined, mat1[...], NN)
     lift_ref[:, :f] = value
-    lift_ref[:, f:] = pick_right(value, whole)
+    lift_ref[:, f:] = pick_right(value, whole, 1)
     own_at = pl.ds(pl.multiple_of(me * count, 8), count)
     mine = mat1[own_at, :]
     own_ref[:, :f] = -mine
-    own_ref[:, f:] = -pick_right(mine, whole)
+    own_ref[:, f:] = -pick_right(mine, whole, 1)
     y_ref[...] = -gx_ref[0, 0, own_at, :]
     rhs[: 2 * m, :] = -xdot(joined, gx_ref[0, 0], NN)
     for h in range(2):
@@ -771,8 +776,10 @@
 
     @pl.loop(0, count_f)
     def _(i):
-        picked = whole_cols(perm_ref, i, f)
-        gx_ref[0, 1, rows_of(i), :] = pick_left(picked, gx_ref[0, 0], 0)
+        picked = (
+            perm_ref[...] == lax.broadcasted_iota(jnp.int32, (BLOCK, f), 0) + i * BLOCK
+        ).astype(jnp.bfloat16)
+        gx_ref[0, 1, rows_of(i), :] = pick_left(picked, gx_ref[0, 0])
 
     tick()
     swap(0).wait_recv()
@@ -822,12 +829,6 @@
     for i in range(len(bulk)):
         for stage in range(-1, last):
             cross(i, stage).wait()
-
-
-def whole_cols(perm_ref, i, f):
-    return (
-        perm_ref[...] == lax.broadcasted_iota(jnp.int32, (f, BLOCK), 1) + i * BLOCK
-    ).astype(jnp.bfloat16)
 
 
 def product_kernel(
@@ -942,7 +943,7 @@
                 (2, 16, *split, count, f),
             )
         ],
-        in_specs=[vmem, vmem],
+        in_specs=[vmem, pl.BlockSpec(memory_space=pl.ANY)],
         out_specs=[vmem] * 5 + [pl.BlockSpec(memory_space=pl.ANY)],
         scratch_shapes=[
             pltpu.VMEM((6, *split, count, f), f32),
@@ -957,7 +958,8 @@
             pltpu.VMEM((3, f, f), f32),
             pltpu.VMEM((rows, 2 * f), f32),
             pltpu.VMEM((f, f), f32),
-            dma((22,)),
+            pltpu.VMEM(dtn.shape, f32),
+            dma((23,)),
             dma((6, last)),
             dma((6, last)),
             dma((6, last)),
@@ -970,9 +972,9 @@
             dma((4,)),
         ],
         compiler_params=pltpu.CompilerParams(
-            collective_id=0, has_side_effects=True, vmem_limit_bytes=48 * 1024 * 1024
+            collective_id=0, has_side_effects=True, vmem_limit_bytes=67_043_328
         ),
-    )(interface_perm[0][:, None], dtn)
+    )(interface_perm, dtn)
     bulk_all = bulk_all.reshape(2, 16, f, f)
     half = (lax.axis_index("box") % 2).astype(jnp.int32)
     lane = 2 * f
@@ -1013,7 +1015,7 @@
             jax.ShapeDtypeStruct((count, 16 * f), f32),
             jax.ShapeDtypeStruct((8, count, 16 * f), f32),
         ],
-        compiler_params=pltpu.CompilerParams(vmem_limit_bytes=40 * 1024 * 1024),
+        compiler_params=pltpu.CompilerParams(vmem_limit_bytes=67_043_328),
     )(half[None], z, lift, own, y, gx, dtn, bulk_all)
     return (first[None], second[None], merged[None])
 

time: 148 us -> 145 us (0.980)
  local copies, waits for them, and re-layouts: 6.64 us -> 0 us
  Pallas kernels: 140 us -> 143 us
    unnamed x6 -> x0, local copies, waits for them, and re-layouts: 5.83 us -> none
    pallas_call x1, Pallas kernels: 17.5 us -> 20.4 us  [fast_body(): pl.pallas_call(product_kernel, grid_spec=pltpu.PrefetchScalarGridSpec(num...]
where the time goes in v4:
time: 145 us; the launch traced here: 144 us
  Pallas kernels  143 us (99%)
    pallas_call x1, Pallas kernels, fast_body(): pl.pallas_call(functools.partial(merge_kernel, plan), out_shape=[jax.Shap...  123 us
    pallas_call x1, Pallas kernels, fast_body(): pl.pallas_call(product_kernel, grid_spec=pltpu.PrefetchScalarGridSpec(num...  20.4 us

profile of v4, /device:TPU:15, one launch (start us, length us, event | category | flops | bytes accessed | tf_op | source)
XLA Modules:
  0.0 144.1 jit_solution(15790721119681010788)
XLA Ops:
  0.6 123.1 %shard_map.49 = (f32[216,768]{1,0:T(8,128)}, f32[192,768]{1,0:T(8,128)}, f32[24,768]{1,0:T(8,128)}, f32[24,768]{1,0:T(8,128)}, f32[2,2,384,768]{3,2,1,0:T(8,128)}, /*index=5*/f32[2,16,2,2,2,2,24,384]{7,6,5,4,3,2,1,0:T(8,128)}) custom-call(s32[1,384]{1,0:T(1,128)} %perm_ref.1, f32[2,6,24,2304]{3,2,1,0:T(8,128)} %dtn_ref.1), custom_call_target="tpu_custom_call" | custom-call | tf_op jit(solution)/shard_map/pallas_call | solution.py:933
  123.7 20.4 %shard_map.50 = (f32[24,3840]{1,0:T(8,128)}, f32[24,6144]{1,0:T(8,128)}, f32[8,24,6144]{2,1,0:T(8,128)}) custom-call(s32[1]{0:T(128)} %bitcast.half_ref, f32[216,768]{1,0:T(8,128)} %get-tuple-element.12.z_ref, f32[192,768]{1,0:T(8,128)} %get-tuple-element.13.lift_ref, f32[24,768]{1,0:T(8,128)} %get-tuple-element.14.own_ref, ...), custom_call_target="tpu_custom_call" | custom-call | tf_op jit(solution)/shard_map/pallas_call | solution.py:989

commit v5 on v4

--- a/solution.py
+++ b/solution.py
@@ -605,8 +605,8 @@
 
 
 def merge_kernel(
-    plan, perm_ref, dtn_any, z_ref, lift_ref, own_ref, y_ref, gx_ref, bulk_ref,
-    small, mat1, mat2, mat3, tee, blk, col, edge, ss, part, rhs, hold, dtn_ref,
+    plan, perm_ref, dtn_any, high_ref, low_ref, y_ref, gx_ref, bulk_ref,
+    small, mat1, mat2, mat3, tee, blk, col, edge, ss, part, rhs, hold, dtn_ref, z_ref, lift_ref, own_ref,
     fill_sem, send0, recv0, send1, recv1, send2, recv2, core_send, core_recv, swap_send, swap_recv,
 ):
     n, f, count = plan["n"], plan["f"], plan["count"]
@@ -817,11 +817,38 @@
     second = xdot(xdot(left, tee[...], NN) - rhs[:, f:], mat3[...], NN)
     z_ref[:, f:] = second
     z_ref[:, :f] = -xdot(left, mat2[...], NN) - xdot(second, tee[...], NT)
-    while events:
-        tick()
+    left_over = [event for some in events for event in some]
+    early = [event for event in left_over if event[2] < last]
+    late = [event for event in left_over if event[2] == last]
+    cut = len(late) // 2
+
+    def finish(some):
+        for name, i, stage in some:
+            advance(groups[name], i, stage)
+
+    def left_factors(q):
+        zs = split2(z_ref[...])
+        for k in range(2):
+            here = slice(k * f, (k + 1) * f)
+            value = -dot3(zs, split2(gx_ref[q, k]), NT)
+            if q == 0:
+                value = jnp.concatenate([value[: 2 * m] + lift_ref[:, here], value[2 * m :]], axis=0)
+            high_ref[q, k, :, :f], low_ref[q, k, :, :f] = split2(
+                jnp.concatenate([value, own_ref[:, here]], axis=0)
+            )
+            high_ref[q, k, :, f:], low_ref[q, k, :, f:] = split2(
+                jnp.concatenate([z_ref[:, here], jnp.zeros((count, f), jnp.float32)], axis=0)
+            )
+
+    finish(early)
+    left_factors(0)
+    finish(late[:cut])
+    gx_copy.wait_recv()
+    left_factors(1)
+    finish(late[cut:])
     for b in range(3):
         swap(b).wait_send()
-    gx_copy.wait()
+    gx_copy.wait_send()
     for group in (first, rest, bulk):
         for g in group:
             for stage in range(last):
@@ -832,33 +859,14 @@
 
 
 def product_kernel(
-    half_ref, z_ref, lift_ref, own_ref, y_ref, gx_ref, dtn_ref, wide_ref,
-    first_ref, second_ref, map_ref, high, low,
+    half_ref, high_ref, low_ref, y_ref, dtn_ref, wide_ref, first_ref, second_ref, map_ref,
 ):
     step = pl.program_id(0)
     q, h, c = step // 4, (step // 2) % 2, 2 * (step % 2)
     half = half_ref[0]
-    rows, f = z_ref.shape[0], z_ref.shape[1] // 2
-    count = own_ref.shape[0]
+    count, f = y_ref.shape[0], y_ref.shape[1] // 2
     m = 4 * count
-
-    @pl.when(step % 4 == 0)
-    def _():
-        z = split2(z_ref[...])
-        for k in range(2):
-            high[k, :rows, f:], low[k, :rows, f:] = [one[:, k * f : (k + 1) * f] for one in z]
-            zero = jnp.zeros((count, f), jnp.bfloat16)
-            high[k, rows:, f:], low[k, rows:, f:] = zero, zero
-            value = -dot3(z, split2(gx_ref[0, k]), NT)
-            high[k, :rows, :f], low[k, :rows, :f] = split2(value)
-
-            @pl.when(q == 0)
-            def _():
-                a, b = split2(value[: 2 * m] + lift_ref[:, k * f : (k + 1) * f])
-                high[k, : 2 * m, :f], low[k, : 2 * m, :f] = a, b
-
-            a, b = split2(own_ref[:, k * f : (k + 1) * f])
-            high[k, rows:, :f], low[k, rows:, :f] = a, b
+    rows = 9 * count
 
     @pl.when(step == 0)
     def _():
@@ -870,7 +878,7 @@
         return wide_ref[0, 2 * k : 2 * k + 2].reshape(2 * f, f)
 
     right = split2(jnp.concatenate([columns(0), columns(1)], axis=1))
-    res = dot3((high[h], low[h]), right, NN)
+    res = dot3((high_ref[0, h], low_ref[0, h]), right, NN)
     map_ref[...] = res[: 2 * m].reshape(map_ref.shape)
     second_ref[...] = res[2 * m : rows]
 
@@ -930,21 +938,20 @@
     dma = pltpu.SemaphoreType.DMA
     rows = 9 * count
     f32 = jnp.float32
-    z, lift, own, y, gx, bulk_all = pl.pallas_call(
+    high, low, y, _, bulk_all = pl.pallas_call(
         functools.partial(merge_kernel, plan),
         out_shape=[
-            jax.ShapeDtypeStruct(s, f32)
-            for s in (
-                (rows, 2 * f),
-                (8 * count, 2 * f),
-                (count, 2 * f),
-                (count, 2 * f),
-                (2, 2, f, 2 * f),
-                (2, 16, *split, count, f),
+            jax.ShapeDtypeStruct(s, kind)
+            for s, kind in (
+                ((2, 2, rows + count, 2 * f), jnp.bfloat16),
+                ((2, 2, rows + count, 2 * f), jnp.bfloat16),
+                ((count, 2 * f), f32),
+                ((2, 2, f, 2 * f), f32),
+                ((2, 16, *split, count, f), f32),
             )
         ],
         in_specs=[vmem, pl.BlockSpec(memory_space=pl.ANY)],
-        out_specs=[vmem] * 5 + [pl.BlockSpec(memory_space=pl.ANY)],
+        out_specs=[vmem] * 4 + [pl.BlockSpec(memory_space=pl.ANY)],
         scratch_shapes=[
             pltpu.VMEM((6, *split, count, f), f32),
             pltpu.VMEM((f, f), f32),
@@ -959,6 +966,9 @@
             pltpu.VMEM((rows, 2 * f), f32),
             pltpu.VMEM((f, f), f32),
             pltpu.VMEM(dtn.shape, f32),
+            pltpu.VMEM((rows, 2 * f), f32),
+            pltpu.VMEM((8 * count, 2 * f), f32),
+            pltpu.VMEM((count, 2 * f), f32),
             dma((23,)),
             dma((6, last)),
             dma((6, last)),
@@ -992,11 +1002,9 @@
             num_scalar_prefetch=1,
             grid=(8,),
             in_specs=[
-                fixed((rows, lane)),
-                fixed((8 * count, lane)),
+                pl.BlockSpec((1, 2, rows + count, lane), lambda s, r: (s // 4, 0, 0, 0)),
+                pl.BlockSpec((1, 2, rows + count, lane), lambda s, r: (s // 4, 0, 0, 0)),
                 fixed((count, lane)),
-                fixed((count, lane)),
-                pl.BlockSpec((1, 2, f, lane), lambda s, r: (s // 4, 0, 0, 0)),
                 fixed(dtn.shape),
                 pl.BlockSpec((1, 4, f, f), lambda s, r: (s // 4, s % 4, 0, 0)),
             ],
@@ -1005,10 +1013,6 @@
                 pl.BlockSpec((count, lane), lambda s, r: (0, column(s, r))),
                 pl.BlockSpec((8, count, lane), lambda s, r: (0, 0, column(s, r))),
             ],
-            scratch_shapes=[
-                pltpu.VMEM((2, rows + count, 2 * f), jnp.bfloat16),
-                pltpu.VMEM((2, rows + count, 2 * f), jnp.bfloat16),
-            ],
         ),
         out_shape=[
             jax.ShapeDtypeStruct((count, 10 * f), f32),
@@ -1016,7 +1020,7 @@
             jax.ShapeDtypeStruct((8, count, 16 * f), f32),
         ],
         compiler_params=pltpu.CompilerParams(vmem_limit_bytes=67_043_328),
-    )(half[None], z, lift, own, y, gx, dtn, bulk_all)
+    )(half[None], high, low, y, dtn, bulk_all)
     return (first[None], second[None], merged[None])
 
 

time: 145 us -> 141 us (0.972)
  Pallas kernels: 143 us -> 140 us
    pallas_call x1, Pallas kernels: 20.4 us -> 15.9 us  [fast_body(): pl.pallas_call(product_kernel, grid_spec=pltpu.PrefetchScalarGridSpec(num...]
where the time goes in v5:
time: 141 us; the launch traced here: 140 us
  Pallas kernels  140 us (99%)
    pallas_call x1, Pallas kernels, fast_body(): pl.pallas_call(functools.partial(merge_kernel, plan), out_shape=[jax.Shap...  124 us
    pallas_call x1, Pallas kernels, fast_body(): pl.pallas_call(product_kernel, grid_spec=pltpu.PrefetchScalarGridSpec(num...  15.9 us

profile of v5, /device:TPU:15, one launch (start us, length us, event | category | flops | bytes accessed | tf_op | source)
XLA Modules:
  0.0 140.2 jit_solution(13091150055835590086)
XLA Ops:
  0.6 123.6 %shard_map.49 = (bf16[2,2,240,768]{3,2,1,0:T(8,128)(2,1)}, bf16[2,2,240,768]{3,2,1,0:T(8,128)(2,1)}, f32[24,768]{1,0:T(8,128)}, f32[2,2,384,768]{3,2,1,0:T(8,128)}, f32[2,16,2,2,2,2,24,384]{7,6,5,4,3,2,1,0:T(8,128)}) custom-call(s32[1,384]{1,0:T(1,128)} %perm_ref.1, f32[2,6,24,2304]{3,2,1,0:T(8,128)} %dtn_ref.1), custom_call_target="tpu_custom_call" | custom-call | tf_op jit(solution)/shard_map/pallas_call | solution.py:941
  124.3 15.9 %shard_map.50 = (f32[24,3840]{1,0:T(8,128)}, f32[24,6144]{1,0:T(8,128)}, f32[8,24,6144]{2,1,0:T(8,128)}) custom-call(s32[1]{0:T(128)} %bitcast.half_ref, bf16[2,2,240,768]{3,2,1,0:T(8,128)(2,1)} %get-tuple-element.10.high_ref, bf16[2,2,240,768]{3,2,1,0:T(8,128)(2,1)} %get-tuple-element.11.low_ref, f32[24,768]{1,0:T(8,128)} %get-tuple-element.12.y_ref, ...), custom_call_target="tpu_custom_call" | custom-call | tf_op jit(solution)/shard_map/pallas_call | solution.py:999
